TPU v7x, 512 devices: a whole 4x8x8 slice. The times are simulated.
512 devices in a mesh: row: 8 (over y), col: 16 (over z, core), rep: 4 (over x).
Axes of the slice: x: 4, y: 8, z: 8, core: 2. Of those that a mesh axis runs over, the one named last changes fastest.
Arguments:
- p_values: float32 [256, 4, 12, 128, 128], P(('row', 'col'), 'rep'), may hold values from -2.5 to 2.5
- p_cols: int32 [1024, 12], replicated, may hold values from 0 to 1023, as said below
- out_cols: int32 [1024, 8], P(('row', 'col')), may hold values from 0 to 1023, as said below
Outputs:
- square: float32 [1024, 8, 128, 128], P(('row', 'col', 'rep'))
Inputs may be any that keep to these rules, and one draw needn't show every extreme that they name: `p_cols`: block row r names 12 distinct block columns c with r - 16 <= c < r + 16; its slots l * 3 to (l + 1) * 3 - 1 hold exactly the 3 columns that are congruent to l modulo 4. `out_cols`: block row r names 8 distinct block columns c with r - 16 <= c <= r + 16.
All inputs are finite; a program needn't handle non-finite values.
Results may differ from a plain program's by a relative error of at most 0.0003.
Values sent between devices are 32-bit elements; how exact they have to be, the bound alone decides.
No kernel may reach another device: no remote copies, remote signals or barrier semaphores. Data moves between devices by JAX's collectives and lax.ppermute only.
A program may use at most 64 MiB of HBM per device.

v0:
```python
import jax
import jax.numpy as jnp
from jax import lax
from jax.sharding import PartitionSpec as P

HIGHEST = lax.Precision.HIGHEST


def passed_along(x, axis, by):
    peers = lax.axis_size(axis)
    pairs = [(i, i + by) for i in range(peers) if 0 <= i + by < peers]
    return lax.ppermute(x, axis, pairs)


def on_device(p_values, p_cols, out_cols):
    layers = lax.axis_size("rep")
    layer_index = lax.axis_index("rep")
    segment = lax.axis_index(("row", "col"))
    own_rows = p_values[:, 0]
    row_count = own_rows.shape[0]
    slot_total = own_rows.shape[1]
    block_size = own_rows.shape[2]
    per_layer = slot_total // layers
    seg_rows = row_count * layers
    gathered = lax.all_gather(p_values, "rep", axis=1, tiled=True)
    entries = lax.dynamic_slice_in_dim(gathered, layer_index * per_layer, per_layer, 2)
    entries = entries.reshape(seg_rows, per_layer, block_size, block_size)
    received = []
    for offset in (2, 1, -1, -2):
        received.append(passed_along(own_rows, ("row", "col"), offset))
    window_rows = jnp.concatenate(
        [received[0], received[1], own_rows, received[2], received[3]], axis=0
    )
    inner_cols = lax.dynamic_slice(
        p_cols, (segment * seg_rows, layer_index * per_layer), (seg_rows, per_layer)
    )
    far_cols = p_cols[inner_cols]
    slot_ids = jnp.arange(slot_total, dtype=jnp.int32)
    matches = far_cols[:, :, None, :] == out_cols[:, None, :, None]
    slot_index = jnp.sum(jnp.where(matches, slot_ids, 0), axis=3)
    present = jnp.any(matches, axis=3)
    window_idx = inner_cols // layers - (segment - 2) * row_count

    def one_row(row_index):
        picked = window_rows[window_idx[row_index][:, None], slot_index[row_index]]
        picked = jnp.where(present[row_index][:, :, None, None], picked, jnp.zeros_like(picked))
        return jnp.einsum("sab,sfbc->fac", entries[row_index], picked, precision=HIGHEST)

    return lax.psum_scatter(
        lax.map(one_row, jnp.arange(row_count * lax.axis_size("rep"), dtype=jnp.int32)),
        "rep",
        scatter_dimension=0,
        tiled=True,
    )


def solution(mesh):
    in_specs = (P(("row", "col"), "rep", None, None, None), P(), P(("row", "col"), None))
    out_specs = P(("row", "col", "rep"), None, None, None)
    return jax.shard_map(
        on_device, mesh=mesh, in_specs=in_specs, out_specs=out_specs, check_vma=False
    )
```

profile of v0, /device:TPU:1, one launch (start us, length us, event | category | flops | bytes accessed | tf_op | source)
XLA Modules:
  0.0 234.3 jit_solution(4974504850985986855)
XLA Ops:
  7.3 6.0 %collective-permute-start = (f32[2,12,128,128]{3,2,1,0:T(8,128)}, f32[2,12,128,128]{3,2,1,0:T(8,128)}, u32[]{:S(2)}, u32[]{:S(2)}) collective-permute-start(f32[2,12,128,128]{3,2,1,0:T(8,128)} %bitcast.41), channel_id=1, source_target_pairs={{0,8},{4,12},{8,16},{12,20},{16,24},{20,28},{24,32},{28,36},{32,40... | collective-permute-start | bytes 4718600 | tf_op jit(solution)/shard_map/ppermute | solution.py:12
  13.3 3.7 %collective-permute-start.1 = (f32[2,12,128,128]{3,2,1,0:T(8,128)}, f32[2,12,128,128]{3,2,1,0:T(8,128)}, u32[]{:S(2)}, u32[]{:S(2)}) collective-permute-start(f32[2,12,128,128]{3,2,1,0:T(8,128)} %bitcast.42), channel_id=1, source_target_pairs={{0,4},{4,8},{8,12},{12,16},{16,20},{20,24},{24,28},{28,32},{32,36}... | collective-permute-start | bytes 4718600 | tf_op jit(solution)/shard_map/ppermute | solution.py:12
  17.0 4.0 %collective-permute-start.2 = (f32[2,12,128,128]{3,2,1,0:T(8,128)}, f32[2,12,128,128]{3,2,1,0:T(8,128)}, u32[]{:S(2)}, u32[]{:S(2)}) collective-permute-start(f32[2,12,128,128]{3,2,1,0:T(8,128)} %bitcast.43), channel_id=1, source_target_pairs={{4,0},{8,4},{12,8},{16,12},{20,16},{24,20},{28,24},{32,28},{36,32}... | collective-permute-start | bytes 4718600 | tf_op jit(solution)/shard_map/ppermute | solution.py:12
  21.0 1.3 collective-permute-start.3
  22.3 1.9 copy.17
  25.0 1.6 gather_fusion.1
  29.1 13.9 %collective-permute-done = f32[2,12,128,128]{3,2,1,0:T(8,128)} collective-permute-done((f32[2,12,128,128]{3,2,1,0:T(8,128)}, f32[2,12,128,128]{3,2,1,0:T(8,128)}, u32[]{:S(2)}, u32[]{:S(2)}) %collective-permute-start) | collective-permute-done | bytes 1572896 | tf_op jit(solution)/shard_map/ppermute | solution.py:12
  43.1 2.7 %constant_dynamic-update-slice_fusion.5 = f32[10,12,128,128]{3,2,1,0:T(8,128)} fusion(f32[2,12,128,128]{3,2,1,0:T(8,128)} %collective-permute-done), kind=kLoop, calls=%fused_computation.29 | loop fusion | bytes 3145728
  45.8 17.7 %collective-permute-done.1 = f32[2,12,128,128]{3,2,1,0:T(8,128)} collective-permute-done((f32[2,12,128,128]{3,2,1,0:T(8,128)}, f32[2,12,128,128]{3,2,1,0:T(8,128)}, u32[]{:S(2)}, u32[]{:S(2)}) %collective-permute-start.1) | collective-permute-done | bytes 1572896 | tf_op jit(solution)/shard_map/ppermute | solution.py:12
  63.5 2.7 %constant_dynamic-update-slice_fusion.4 = f32[10,12,128,128]{3,2,1,0:T(8,128)} fusion(f32[10,12,128,128]{3,2,1,0:T(8,128)} %constant_dynamic-update-slice_fusion.5, f32[2,12,128,128]{3,2,1,0:T(8,128)} %collective-permute-done.1), kind=kLoop, calls=%fused_computation.28 | loop fusion | bytes 3145728
  67.5 2.7 %constant_dynamic-update-slice_fusion.2 = f32[10,12,128,128]{3,2,1,0:T(8,128)} fusion(f32[10,12,128,128]{3,2,1,0:T(8,128)} %constant_dynamic-update-slice_fusion.3, f32[2,12,128,128]{3,2,1,0:T(8,128)} %collective-permute-done.2), kind=kLoop, calls=%fused_computation.26 | loop fusion | bytes 3145728
  70.2 1.3 constant_dynamic-update-slice_fusion.1
  71.5 14.5 %all-gather.2.cloned.1.call-done = f32[2,4,12,128,128]{4,3,2,1,0:T(8,128)} async-done(((f32[2,1,12,128,128]{4,3,2,1,0:T(8,128)}), f32[2,4,12,128,128]{4,3,2,1,0:T(8,128)}) %all-gather.2.cloned.1.call-update) | async-done | bytes 6291472 | tf_op jit(solution)/shard_map/all_gather | solution.py:25
  86.0 2.7 %constant_dynamic-slice_fusion.1 = f32[2,4,3,128,128]{4,3,2,1,0:T(8,128)} fusion(f32[2,4,12,128,128]{4,3,2,1,0:T(8,128)} %all-gather.2.cloned.1.call-done, s32[]{:T(128)S(6)} %select_n.48), kind=kLoop, calls=%fused_computation.40 | loop fusion | bytes 3145732 | tf_op jit(solution)/shard_map/dynamic_slice | solution.py:26
  88.7 85.6 %while.10 = (s32[]{:T(128)}, f32[8,8,128,128]{3,2,1,0:T(8,128)}, s32[8]{0:T(128)S(1)}, pred[8,3,8]{2,1,0:T(4,128)(4,1)S(1)}, s32[8,3]{1,0:T(8,128)S(1)}, /*index...) while((s32[]{:T(128)}, f32[8,8,128,128]{3,2,1,0:T(8,128)}, ...), condition=%wide.region_3.4_spmd, body=%wide.region_2.3_spmd.sunk | while | flops 604373184 | bytes 10683783 | solution.py:50
  91.4 3.9 %gather_fusion = f32[24,128,128]{2,1,0:T(8,128)S(1)} fusion(f32[10,12,128,128]{3,2,1,0:T(8,128)} %get-tuple-element.151, s32[24]{0:T(128)S(1)} %reshape.83), kind=kCustom, calls=%fused_computation.clone.1 | custom fusion | bytes 3145920 | tf_op jit(solution)/shard_map/while/body/eval_jaxpr/gather | solution.py:45
  95.9 2.4 %fusion.27 = f32[1,8,128,128]{2,3,1,0:T(8,128)S(1)} fusion(f32[3,8,128,128]{2,3,0,1:T(8,128)S(1)} %copy.26, pred[3,8]{0,1:T(8,128)(4,1)S(1)} %copy.27, f32[8,3,128,128]{3,2,1,0:T(8,128)} %get-tuple-element.152, s32[]{:T(128)S(6)} %select_n.82), kind=kOutput, calls=%fused_computation.4.clone.1 | convolution fusion | flops 604372992 | bytes 2293788 | tf_op jit(solution)/shard_map/while/body/eval_jaxpr/sab,sfbc->fac/dot_general | solution.py:47
  102.1 3.9 %gather_fusion = f32[24,128,128]{2,1,0:T(8,128)S(1)} fusion(f32[10,12,128,128]{3,2,1,0:T(8,128)} %get-tuple-element.151, s32[24]{0:T(128)S(1)} %reshape.83), kind=kCustom, calls=%fused_computation.clone.1 | custom fusion | bytes 3145920 | tf_op jit(solution)/shard_map/while/body/eval_jaxpr/gather | solution.py:45
  106.6 2.4 %fusion.27 = f32[1,8,128,128]{2,3,1,0:T(8,128)S(1)} fusion(f32[3,8,128,128]{2,3,0,1:T(8,128)S(1)} %copy.26, pred[3,8]{0,1:T(8,128)(4,1)S(1)} %copy.27, f32[8,3,128,128]{3,2,1,0:T(8,128)} %get-tuple-element.152, s32[]{:T(128)S(6)} %select_n.82), kind=kOutput, calls=%fused_computation.4.clone.1 | convolution fusion | flops 604372992 | bytes 2293788 | tf_op jit(solution)/shard_map/while/body/eval_jaxpr/sab,sfbc->fac/dot_general | solution.py:47
  112.8 3.9 %gather_fusion = f32[24,128,128]{2,1,0:T(8,128)S(1)} fusion(f32[10,12,128,128]{3,2,1,0:T(8,128)} %get-tuple-element.151, s32[24]{0:T(128)S(1)} %reshape.83), kind=kCustom, calls=%fused_computation.clone.1 | custom fusion | bytes 3145920 | tf_op jit(solution)/shard_map/while/body/eval_jaxpr/gather | solution.py:45
  117.3 2.4 %fusion.27 = f32[1,8,128,128]{2,3,1,0:T(8,128)S(1)} fusion(f32[3,8,128,128]{2,3,0,1:T(8,128)S(1)} %copy.26, pred[3,8]{0,1:T(8,128)(4,1)S(1)} %copy.27, f32[8,3,128,128]{3,2,1,0:T(8,128)} %get-tuple-element.152, s32[]{:T(128)S(6)} %select_n.82), kind=kOutput, calls=%fused_computation.4.clone.1 | convolution fusion | flops 604372992 | bytes 2293788 | tf_op jit(solution)/shard_map/while/body/eval_jaxpr/sab,sfbc->fac/dot_general | solution.py:47
  123.5 3.9 %gather_fusion = f32[24,128,128]{2,1,0:T(8,128)S(1)} fusion(f32[10,12,128,128]{3,2,1,0:T(8,128)} %get-tuple-element.151, s32[24]{0:T(128)S(1)} %reshape.83), kind=kCustom, calls=%fused_computation.clone.1 | custom fusion | bytes 3145920 | tf_op jit(solution)/shard_map/while/body/eval_jaxpr/gather | solution.py:45
  128.0 2.4 %fusion.27 = f32[1,8,128,128]{2,3,1,0:T(8,128)S(1)} fusion(f32[3,8,128,128]{2,3,0,1:T(8,128)S(1)} %copy.26, pred[3,8]{0,1:T(8,128)(4,1)S(1)} %copy.27, f32[8,3,128,128]{3,2,1,0:T(8,128)} %get-tuple-element.152, s32[]{:T(128)S(6)} %select_n.82), kind=kOutput, calls=%fused_computation.4.clone.1 | convolution fusion | flops 604372992 | bytes 2293788 | tf_op jit(solution)/shard_map/while/body/eval_jaxpr/sab,sfbc->fac/dot_general | solution.py:47
  134.2 3.9 %gather_fusion = f32[24,128,128]{2,1,0:T(8,128)S(1)} fusion(f32[10,12,128,128]{3,2,1,0:T(8,128)} %get-tuple-element.151, s32[24]{0:T(128)S(1)} %reshape.83), kind=kCustom, calls=%fused_computation.clone.1 | custom fusion | bytes 3145920 | tf_op jit(solution)/shard_map/while/body/eval_jaxpr/gather | solution.py:45
  138.7 2.4 %fusion.27 = f32[1,8,128,128]{2,3,1,0:T(8,128)S(1)} fusion(f32[3,8,128,128]{2,3,0,1:T(8,128)S(1)} %copy.26, pred[3,8]{0,1:T(8,128)(4,1)S(1)} %copy.27, f32[8,3,128,128]{3,2,1,0:T(8,128)} %get-tuple-element.152, s32[]{:T(128)S(6)} %select_n.82), kind=kOutput, calls=%fused_computation.4.clone.1 | convolution fusion | flops 604372992 | bytes 2293788 | tf_op jit(solution)/shard_map/while/body/eval_jaxpr/sab,sfbc->fac/dot_general | solution.py:47
  144.9 3.9 %gather_fusion = f32[24,128,128]{2,1,0:T(8,128)S(1)} fusion(f32[10,12,128,128]{3,2,1,0:T(8,128)} %get-tuple-element.151, s32[24]{0:T(128)S(1)} %reshape.83), kind=kCustom, calls=%fused_computation.clone.1 | custom fusion | bytes 3145920 | tf_op jit(solution)/shard_map/while/body/eval_jaxpr/gather | solution.py:45
  149.4 2.4 %fusion.27 = f32[1,8,128,128]{2,3,1,0:T(8,128)S(1)} fusion(f32[3,8,128,128]{2,3,0,1:T(8,128)S(1)} %copy.26, pred[3,8]{0,1:T(8,128)(4,1)S(1)} %copy.27, f32[8,3,128,128]{3,2,1,0:T(8,128)} %get-tuple-element.152, s32[]{:T(128)S(6)} %select_n.82), kind=kOutput, calls=%fused_computation.4.clone.1 | convolution fusion | flops 604372992 | bytes 2293788 | tf_op jit(solution)/shard_map/while/body/eval_jaxpr/sab,sfbc->fac/dot_general | solution.py:47
  155.6 3.9 %gather_fusion = f32[24,128,128]{2,1,0:T(8,128)S(1)} fusion(f32[10,12,128,128]{3,2,1,0:T(8,128)} %get-tuple-element.151, s32[24]{0:T(128)S(1)} %reshape.83), kind=kCustom, calls=%fused_computation.clone.1 | custom fusion | bytes 3145920 | tf_op jit(solution)/shard_map/while/body/eval_jaxpr/gather | solution.py:45
  160.1 2.4 %fusion.27 = f32[1,8,128,128]{2,3,1,0:T(8,128)S(1)} fusion(f32[3,8,128,128]{2,3,0,1:T(8,128)S(1)} %copy.26, pred[3,8]{0,1:T(8,128)(4,1)S(1)} %copy.27, f32[8,3,128,128]{3,2,1,0:T(8,128)} %get-tuple-element.152, s32[]{:T(128)S(6)} %select_n.82), kind=kOutput, calls=%fused_computation.4.clone.1 | convolution fusion | flops 604372992 | bytes 2293788 | tf_op jit(solution)/shard_map/while/body/eval_jaxpr/sab,sfbc->fac/dot_general | solution.py:47
  166.3 3.9 %gather_fusion = f32[24,128,128]{2,1,0:T(8,128)S(1)} fusion(f32[10,12,128,128]{3,2,1,0:T(8,128)} %get-tuple-element.151, s32[24]{0:T(128)S(1)} %reshape.83), kind=kCustom, calls=%fused_computation.clone.1 | custom fusion | bytes 3145920 | tf_op jit(solution)/shard_map/while/body/eval_jaxpr/gather | solution.py:45
  170.8 2.4 %fusion.27 = f32[1,8,128,128]{2,3,1,0:T(8,128)S(1)} fusion(f32[3,8,128,128]{2,3,0,1:T(8,128)S(1)} %copy.26, pred[3,8]{0,1:T(8,128)(4,1)S(1)} %copy.27, f32[8,3,128,128]{3,2,1,0:T(8,128)} %get-tuple-element.152, s32[]{:T(128)S(6)} %select_n.82), kind=kOutput, calls=%fused_computation.4.clone.1 | convolution fusion | flops 604372992 | bytes 2293788 | tf_op jit(solution)/shard_map/while/body/eval_jaxpr/sab,sfbc->fac/dot_general | solution.py:47
  174.3 53.1 %reduce-scatter.2.cloned.1.call-done = f32[2,8,128,128]{3,2,1,0:T(8,128)} async-done(((f32[8,8,128,128]{3,2,1,0:T(8,128)}), f32[2,8,128,128]{3,2,1,0:T(8,128)}) %reduce-scatter.2.cloned.1.call-update) | async-done | bytes 1048592 | tf_op jit(solution)/shard_map/reduce_scatter | solution.py:49
  (90 shorter events, 24.4 us)
Async XLA Ops:
  6.5 59.7 %copy-start = (f32[2,1,12,128,128]{4,3,2,1,0:T(8,128)S(1)}, f32[2,1,12,128,128]{4,3,2,1,0:T(8,128)}, u32[]{:S(2)}) copy-start(f32[2,1,12,128,128]{4,3,2,1,0:T(8,128)} %param.5) | copy-start | bytes 4718596
  6.5 79.4 %all-gather.2.cloned.1.call-start = ((), (), s32[]{:S(2)}) async-start(), calls=%async_computation.1 | async-start | bytes 7864320 | tf_op jit(solution)/shard_map/all_gather | solution.py:25
  7.3 220.2 %reduce-scatter.2.cloned.1.call-start = ((), (), s32[]{:S(2)}) async-start(), calls=%async_computation.2 | async-start | bytes 5242880 | tf_op jit(solution)/shard_map/reduce_scatter | solution.py:49
  7.3 35.8 %collective-permute-start = (f32[2,12,128,128]{3,2,1,0:T(8,128)}, f32[2,12,128,128]{3,2,1,0:T(8,128)}, u32[]{:S(2)}, u32[]{:S(2)}) collective-permute-start(f32[2,12,128,128]{3,2,1,0:T(8,128)} %bitcast.41), channel_id=1, source_target_pairs={{0,8},{4,12},{8,16},{12,20},{16,24},{20,28},{24,32},{28,36},{32,40... | collective-permute-start | bytes 4718600 | tf_op jit(solution)/shard_map/ppermute | solution.py:12
  13.3 50.2 %collective-permute-start.1 = (f32[2,12,128,128]{3,2,1,0:T(8,128)}, f32[2,12,128,128]{3,2,1,0:T(8,128)}, u32[]{:S(2)}, u32[]{:S(2)}) collective-permute-start(f32[2,12,128,128]{3,2,1,0:T(8,128)} %bitcast.42), channel_id=1, source_target_pairs={{0,4},{4,8},{8,12},{12,16},{16,20},{20,24},{24,28},{28,32},{32,36}... | collective-permute-start | bytes 4718600 | tf_op jit(solution)/shard_map/ppermute | solution.py:12
  17.0 50.5 %collective-permute-start.2 = (f32[2,12,128,128]{3,2,1,0:T(8,128)}, f32[2,12,128,128]{3,2,1,0:T(8,128)}, u32[]{:S(2)}, u32[]{:S(2)}) collective-permute-start(f32[2,12,128,128]{3,2,1,0:T(8,128)} %bitcast.43), channel_id=1, source_target_pairs={{4,0},{8,4},{12,8},{16,12},{20,16},{24,20},{28,24},{32,28},{36,32}... | collective-permute-start | bytes 4718600 | tf_op jit(solution)/shard_map/ppermute | solution.py:12
  21.0 49.2 %collective-permute-start.3 = (f32[2,12,128,128]{3,2,1,0:T(8,128)}, f32[2,12,128,128]{3,2,1,0:T(8,128)S(1)}, u32[]{:S(2)}, u32[]{:S(2)}) collective-permute-start(f32[2,12,128,128]{3,2,1,0:T(8,128)} %bitcast.44), channel_id=1, source_target_pairs={{8,0},{12,4},{16,8},{20,12},{24,16},{28,20},{32,24},{36,28},{40,32... | collective-permute-start | bytes 4718600 | tf_op jit(solution)/shard_map/ppermute | solution.py:12
Sparse Core Ops, SparseCore 0:
  9.5 76.4 all-gather.1
  174.4 52.9 reduce-scatter.1
where the time goes:
time: 235 us; the launch traced here: 234 us
  waiting for transfers between devices  100 us (43%)
  local copies, waits for them, and re-layouts  66.4 us (28%)
  matrix products  19.4 us (8%)
  loops' own time  15.9 us (7%)
  starting transfers between devices  15 us (6%)
  between operations  13.5 us (6%)
  other arithmetic  4.07 us (2%)
    reduce_scatter x1, waiting for transfers between devices, on_device(): lax.psum_scatter(lax.map(one_row, jnp.arange(row_count * lax.axis_size('r...  53.1 us
    gather x16, local copies, waits for them, and re-layouts, one_row(): picked = window_rows[window_idx[row_index][:, None], slot_index[row_index]]  34.9 us
    ppermute x4, waiting for transfers between devices, passed_along(): return lax.ppermute(x, axis, pairs)  31.6 us
    dot_general x8, matrix products, one_row(): jnp.einsum('sab,sfbc->fac', entries[row_index], picked, precision=HIGHEST)  19.4 us
    another operation x1, loops' own time, on_device(): lax.map(one_row, jnp.arange(row_count * lax.axis_size('rep'), dtype=jnp.i...  15.9 us
    ppermute x4, starting transfers between devices, passed_along(): return lax.ppermute(x, axis, pairs)  15 us
    all_gather x1, waiting for transfers between devices, on_device(): gathered = lax.all_gather(p_values, 'rep', axis=1, tiled=True)  14.5 us
    unnamed x7, local copies, waits for them, and re-layouts  11.3 us
  transfers between devices with their start and end apart: 6, of which 4 were waited for; matrix products, arithmetic and copies ran while one was open for 7% of the time, Pallas kernels for 0%

commit v1 on v0

v1 whole, which is shorter than its diff:
```python
import functools

import jax
import jax.numpy as jnp
from jax import lax
from jax.experimental import pallas as pl
from jax.experimental.pallas import tpu as pltpu
from jax.sharding import PartitionSpec as P

HALF = 64
SEG = ("row", "col")


def roll_half(x):
    return pltpu.roll(x, HALF, x.ndim - 1)


def left_lanes(shape):
    return lax.broadcasted_iota(jnp.int32, shape, len(shape) - 1) < HALF


def prepare_body(layer, own, half0, half1, part0, part1, part2, part3):
    pairs = half0.shape[1]
    layers = 4
    per_layer = part0.shape[1]
    for t in range(pairs):
        low, high = own[0, t], own[0, t + pairs]
        left = left_lanes(low.shape)
        half0[0, t] = jnp.where(left, low, roll_half(high))
        half1[0, t] = jnp.where(left, roll_half(low), high)
    for step, part in enumerate((part0, part1, part2, part3)):
        first = lax.rem(layer[0] + step, layers) * per_layer
        part[0] = own[0, pl.ds(first, per_layer)]


def prepare(layer, own):
    rows, slots, size, _ = own.shape
    pairs, per_layer = slots // 2, slots // 4
    half = jax.ShapeDtypeStruct((rows, pairs, size, size), own.dtype)
    part = jax.ShapeDtypeStruct((rows, per_layer, size, size), own.dtype)

    def spec(count):
        return pl.BlockSpec((1, count, size, size), lambda q, _: (q, 0, 0, 0))

    return pl.pallas_call(
        prepare_body,
        grid_spec=pltpu.PrefetchScalarGridSpec(
            num_scalar_prefetch=1,
            grid=(rows,),
            in_specs=[spec(slots)],
            out_specs=[spec(pairs)] * 2 + [spec(per_layer)] * 4,
        ),
        out_shape=[half] * 2 + [part] * 4,
        compiler_params=pltpu.CompilerParams(vmem_limit_bytes=24 << 20),
        cost_estimate=pl.CostEstimate(flops=0, transcendentals=0, bytes_accessed=5 << 20),
        name="prepare",
    )(layer, own)


def split(x):
    high = x.astype(jnp.bfloat16)
    return high, (x - high.astype(jnp.float32)).astype(jnp.bfloat16)


def product_body(where, layer, *refs):
    parts, windows, outs = refs[:4], refs[4:9], refs[9:13]
    a_high, a_low, w_high, w_low, p_high, p_low = refs[13:]
    rows, per_layer, size, _ = parts[0].shape
    pairs = windows[0].shape[1]
    slots = 2 * pairs
    layers = 4
    out_pairs = outs[0].shape[1]
    none = len(windows) * rows * slots

    for d, part in enumerate(parts):
        for q in range(rows):
            for s in range(per_layer):
                high, low = split(part[q, s])
                cols = slice(s * size, (s + 1) * size)
                a_high[d * rows + q, :, cols] = high
                a_low[d * rows + q, :, cols] = low

    def load_window(b, window):
        for q in range(rows):
            for t in range(pairs):
                x = window[q, t]
                base = (b * rows + q) * slots + t
                high, low = split(x)
                w_high[base], w_low[base] = high, low
                high, low = split(roll_half(x))
                w_high[base + pairs], w_low[base + pairs] = high, low

    for b, window in enumerate(windows):
        load_window(b, window)
    w_high[none] = jnp.zeros((size, size), jnp.bfloat16)
    w_low[none] = jnp.zeros((size, size), jnp.bfloat16)
    left = left_lanes((size, size))
    for d, out in enumerate(outs):
        for i in range(2):
            row = 2 * lax.rem(layer[0] + d, layers) + i
            entry = lax.rem(layer[0] + layers - lax.rem(row, layers), layers) * rows + lax.div(row, layers)
            for s in range(per_layer):
                at = (row * per_layer + s) * 2 * out_pairs
                for p in range(out_pairs):
                    one, two = where[at + p], where[at + out_pairs + p]
                    to = (slice(s * size, (s + 1) * size), slice(p * size, (p + 1) * size))
                    p_high[to] = jnp.where(left, w_high[one], w_high[two])
                    p_low[to] = jnp.where(left, w_low[one], w_low[two])
            dot = functools.partial(jnp.dot, preferred_element_type=jnp.float32)
            high = a_high[entry]
            total = dot(high, p_high[...]) + (dot(high, p_low[...]) + dot(a_low[entry], p_high[...]))
            for p in range(out_pairs):
                out[i, p] = total[:, p * size : (p + 1) * size]


def product(where, layer, parts, windows):
    rows, per_layer, size, _ = parts[0].shape
    pairs = windows[0].shape[1]
    slots = 2 * pairs
    out_pairs = 4
    vmem = pl.BlockSpec(memory_space=pltpu.VMEM)
    smem = pl.BlockSpec(memory_space=pltpu.SMEM)
    blocks = len(windows) * rows * slots + 1
    width = per_layer * size
    return pl.pallas_call(
        product_body,
        in_specs=[smem, smem] + [vmem] * 9,
        out_specs=[vmem] * 4,
        out_shape=[jax.ShapeDtypeStruct((2, out_pairs, size, size), jnp.float32)] * 4,
        scratch_shapes=[pltpu.VMEM((4 * rows, size, width), jnp.bfloat16)] * 2
        + [pltpu.VMEM((blocks, size, size), jnp.bfloat16)] * 2
        + [pltpu.VMEM((width, out_pairs * size), jnp.bfloat16)] * 2,
        compiler_params=pltpu.CompilerParams(vmem_limit_bytes=40 << 20),
        cost_estimate=pl.CostEstimate(flops=2_400_000_000, transcendentals=0, bytes_accessed=8 << 20),
        name="product",
    )(where, layer, *parts, *windows)


def gather_body(*refs):
    out = refs[-1]
    half0, half1 = refs[:4], refs[4:8]
    pairs = half0[0].shape[1]
    for p in range(pairs):
        one = (half0[0][0, p] + half0[1][0, p]) + (half0[2][0, p] + half0[3][0, p])
        two = (half1[0][0, p] + half1[1][0, p]) + (half1[2][0, p] + half1[3][0, p])
        left = left_lanes(one.shape)
        out[0, p] = jnp.where(left, one, roll_half(two))
        out[0, p + pairs] = jnp.where(left, roll_half(one), two)


def add_up(half0, half1):
    rows, pairs, size, _ = half0[0].shape
    spec = pl.BlockSpec((1, pairs, size, size), lambda i: (i, 0, 0, 0))
    return pl.pallas_call(
        gather_body,
        grid=(rows,),
        in_specs=[spec] * 8,
        out_specs=pl.BlockSpec((1, 2 * pairs, size, size), lambda i: (i, 0, 0, 0)),
        out_shape=jax.ShapeDtypeStruct((rows, 2 * pairs, size, size), jnp.float32),
        compiler_params=pltpu.CompilerParams(vmem_limit_bytes=24 << 20),
        cost_estimate=pl.CostEstimate(flops=0, transcendentals=0, bytes_accessed=5 << 20),
        name="add_up",
    )(*half0, *half1)


def find(p_cols, out_cols, segment, layer):
    seg_rows, out_count = out_cols.shape
    total_rows, slots = p_cols.shape
    per_layer = slots // 4
    span = 5 * seg_rows
    first = jnp.clip(segment * seg_rows - 2 * seg_rows, 0, total_rows - span)
    near = lax.dynamic_slice(p_cols, (first, 0), (span, slots))
    inner = lax.dynamic_slice(p_cols, (segment * seg_rows, layer * per_layer), (seg_rows, per_layer))
    at = jnp.arange(span, dtype=jnp.int32)[None, None, :, None]
    far = jnp.sum(jnp.where(inner[:, :, None, None] - first == at, near[None, None], 0), axis=2)
    matches = far[:, :, None, :] == out_cols[:, None, :, None]
    slot_ids = jnp.arange(slots, dtype=jnp.int32)
    slot = jnp.sum(jnp.where(matches, slot_ids + 1, 0), axis=3) - 1
    offset = inner // seg_rows - segment
    even = segment % 2 == 0
    sign = jnp.where(even, offset, -offset)
    source = jnp.where(sign == 0, 0, jnp.where(sign == 1, 1, jnp.where(sign == 2, 2, jnp.where(sign == -2, 3, 4))))
    base = (source * 2 + (inner // 4) % 2) * slots
    swapped = jnp.where(jnp.arange(out_count) < out_count // 2, 0, slots // 2)
    place = (slot + swapped) % slots
    none = 5 * 2 * slots
    return jnp.where(slot >= 0, base[:, :, None] + place, none).reshape(-1)


def on_device(p_values, p_cols, out_cols):
    layers = lax.axis_size("rep")
    layer = lax.axis_index("rep")
    segment = lax.axis_index(SEG)
    segments = lax.axis_size(SEG[0]) * lax.axis_size(SEG[1])
    own = p_values[:, 0]
    layer_ref = layer.reshape(1).astype(jnp.int32)

    def on_segments(x, step):
        pairs = [(i, step(i)) for i in range(segments) if 0 <= step(i) < segments]
        return lax.ppermute(x, SEG, pairs)

    def partner(x):
        return on_segments(x, lambda i: i ^ 1)

    def forwarded(x):
        return on_segments(x, lambda i: i - 2 if i % 2 == 0 else i + 2)

    def kept(x):
        return on_segments(x, lambda i: i + 2 if i % 2 == 0 else i - 2)

    def to_layer(x, step):
        return lax.ppermute(x, "rep", [(i, (i + step) % layers) for i in range(layers)])

    half0, half1, *mine = prepare(layer_ref, own)
    where = find(p_cols, out_cols, segment, layer)

    ahead0 = forwarded(half0)
    behind0 = kept(half0)
    parts = [mine[0]] + [to_layer(mine[step], step) for step in (1, 2, 3)]
    other0, other1 = partner(half0), partner(half1)
    across0 = partner(ahead0)
    half1_later, ahead0, behind0 = lax.optimization_barrier((half1, ahead0, behind0))
    ahead1 = forwarded(half1_later)
    behind1 = kept(half1_later)
    across1 = partner(ahead1)

    def sums(windows):
        shares = product(where, layer_ref, parts, windows)
        return [shares[0]] + [to_layer(shares[step], step) for step in (1, 2, 3)]

    sum0 = sums((half0, other0, ahead0, behind0, across0))
    sum1 = sums((half1, other1, ahead1, behind1, across1))
    return add_up(sum0, sum1)


def solution(mesh):
    in_specs = (P(("row", "col"), "rep", None, None, None), P(), P(("row", "col"), None))
    out_specs = P(("row", "col", "rep"), None, None, None)
    return jax.shard_map(
        on_device, mesh=mesh, in_specs=in_specs, out_specs=out_specs, check_vma=False
    )
```

time: 235 us -> 124 us (0.53)
  the two profiles are of different devices: /device:TPU:1 before, /device:TPU:32 now
where the time goes in v1:
time: 124 us; the launch traced here: 123 us
  starting transfers between devices  60.8 us (49%)
  waiting for transfers between devices  33.2 us (27%)
  Pallas kernels  15.2 us (12%)
  local copies, waits for them, and re-layouts  7.97 us (6%)
  other arithmetic  5.3 us (4%)
    ppermute x8, starting transfers between devices, on_segments(): return lax.ppermute(x, SEG, pairs)  30.5 us
    ppermute x9, starting transfers between devices, to_layer(): lax.ppermute(x, 'rep', [(i, (i + step) % layers) for i in range(layers)])  30.3 us
    ppermute x9, waiting for transfers between devices, to_layer(): lax.ppermute(x, 'rep', [(i, (i + step) % layers) for i in range(layers)])  29.4 us
    pallas_call x2, Pallas kernels, product(): pl.pallas_call(product_body, in_specs=[smem, smem] + [vmem] * 9, out_spec...  12.7 us
    ppermute x8, waiting for transfers between devices, on_segments(): return lax.ppermute(x, SEG, pairs)  3.78 us
  transfers between devices with their start and end apart: 17, of which 5 were waited for; matrix products, arithmetic and copies ran while one was open for 9% of the time, Pallas kernels for 10%

profile of v1, /device:TPU:32, one launch (start us, length us, event | category | flops | bytes accessed | tf_op | source)
XLA Modules:
  0.0 122.8 jit_solution(16737643472610149905)
XLA Ops:
  0.0 1.4 %copy-done = f32[2,1,12,128,128]{4,3,2,1,0:T(8,128)S(1)} copy-done((f32[2,1,12,128,128]{4,3,2,1,0:T(8,128)S(1)}, f32[2,1,12,128,128]{4,3,2,1,0:T(8,128)}, u32[]{:S(2)}) %copy-start) | copy-done | bytes 1572888
  1.4 1.3 %prepare.1 = (f32[2,6,128,128]{3,2,1,0:T(8,128)S(1)}, f32[2,6,128,128]{3,2,1,0:T(8,128)S(1)}, f32[2,3,128,128]{3,2,1,0:T(8,128)S(1)}, f32[2,3,128,128]{3,2,1,0:T...) custom-call(s32[1]{0:T(128)} %bitcast.layer, f32[2,12,128,128]{3,2,1,0:T(8,128)S(1)} %bitcast.2), custom_call_target="tpu_custom_call" | custom-call | bytes 5242880 | tf_op jit(solution)/shard_map/prepare/pallas_call | solution.py:45
  3.4 10.8 %collective-permute-start.4 = (f32[2,6,128,128]{3,2,1,0:T(8,128)S(1)}, f32[2,6,128,128]{3,2,1,0:T(8,128)S(1)}, u32[]{:S(2)}, u32[]{:S(2)}) collective-permute-start(f32[2,6,128,128]{3,2,1,0:T(8,128)S(1)} %get-tuple-element.26.refs_4_), channel_id=1, source_target_pairs={{4,12},{8,0},{12,20},{16,8},{20,28},{24,16},{28,36},{32,24},{36,44... | collective-permute-start | bytes 2359304 | tf_op jit(solution)/shard_map/ppermute | solution.py:200
  14.3 1.9 %collective-permute-start.5 = (f32[2,6,128,128]{3,2,1,0:T(8,128)S(1)}, f32[2,6,128,128]{3,2,1,0:T(8,128)S(1)}, u32[]{:S(2)}, u32[]{:S(2)}) collective-permute-start(f32[2,6,128,128]{3,2,1,0:T(8,128)S(1)} %get-tuple-element.26.refs_4_), channel_id=1, source_target_pairs={{0,8},{8,16},{12,4},{16,24},{20,12},{24,32},{28,20},{32,40},{36,28... | collective-permute-start | bytes 2359304 | tf_op jit(solution)/shard_map/ppermute | solution.py:200
  16.2 1.9 %collective-permute-start.3 = (f32[2,6,128,128]{3,2,1,0:T(8,128)S(1)}, f32[2,6,128,128]{3,2,1,0:T(8,128)}, u32[]{:S(2)}, u32[]{:S(2)}) collective-permute-start(f32[2,6,128,128]{3,2,1,0:T(8,128)S(1)} %get-tuple-element.26.refs_4_), channel_id=1, source_target_pairs={{0,4},{4,0},{8,12},{12,8},{16,20},{20,16},{24,28},{28,24},{32,36},... | collective-permute-start | bytes 2359304 | tf_op jit(solution)/shard_map/ppermute | solution.py:200
  18.1 3.4 %collective-permute-start = (f32[2,3,128,128]{3,2,1,0:T(8,128)}, f32[2,3,128,128]{3,2,1,0:T(8,128)}, u32[]{:S(2)}, u32[]{:S(2)}) collective-permute-start(f32[2,3,128,128]{3,2,1,0:T(8,128)} %get-tuple-element.23), channel_id=1, source_target_pairs={{0,1},{1,2},{2,3},{3,0},{4,5},{5,6},{6,7},{7,4},{8,9},{9,10},{10,1... | collective-permute-start | bytes 1179656 | tf_op jit(solution)/shard_map/ppermute | solution.py:212
  21.5 4.6 %collective-permute-start.1 = (f32[2,3,128,128]{3,2,1,0:T(8,128)}, f32[2,3,128,128]{3,2,1,0:T(8,128)}, u32[]{:S(2)}, u32[]{:S(2)}) collective-permute-start(f32[2,3,128,128]{3,2,1,0:T(8,128)} %get-tuple-element.24), channel_id=1, source_target_pairs={{0,2},{1,3},{2,0},{3,1},{4,6},{5,7},{6,4},{7,5},{8,10},{9,11},{10,... | collective-permute-start | bytes 1179656 | tf_op jit(solution)/shard_map/ppermute | solution.py:212
  26.2 1.4 %fusion.5 = (s32[8,3]{0,1:T(4,128)}, s32[8,3]{0,1:T(4,128)S(1)}) fusion(s32[1024,12]{0,1:T(8,128)} %param.4, s32[]{:T(128)S(6)} %select_n.78, s32[]{:T(128)S(6)} %select_n.79, s32[]{:T(128)S(6)} %add.60, pred[]{:T(512)S(6)} %eq.58, s32[]{:T(128)S(6)} %min.4), kind=kLoop, calls=%fused_computation.21 | loop fusion | flops 1224 | bytes 305 | tf_op jit(solution)/shard_map/mul | solution.py:183
  27.7 3.8 %collective-permute-done.4.refs_6_ = f32[2,6,128,128]{3,2,1,0:T(8,128)S(1)} collective-permute-done((f32[2,6,128,128]{3,2,1,0:T(8,128)S(1)}, f32[2,6,128,128]{3,2,1,0:T(8,128)S(1)}, u32[]{:S(2)}, u32[]{:S(2)}) %collective-permute-start.4) | collective-permute-done | bytes 786464 | tf_op jit(solution)/shard_map/ppermute | solution.py:200
  31.4 4.7 %collective-permute-start.2 = (f32[2,3,128,128]{3,2,1,0:T(8,128)}, f32[2,3,128,128]{3,2,1,0:T(8,128)}, u32[]{:S(2)}, u32[]{:S(2)}) collective-permute-start(f32[2,3,128,128]{3,2,1,0:T(8,128)} %copy-done.1), channel_id=1, source_target_pairs={{0,3},{1,0},{2,1},{3,2},{4,7},{5,4},{6,5},{7,6},{8,11},{9,8},{10,9... | collective-permute-start | bytes 1179656 | tf_op jit(solution)/shard_map/ppermute | solution.py:212
  36.1 7.7 %collective-permute-start.11 = (f32[2,6,128,128]{3,2,1,0:T(8,128)S(1)}, f32[2,6,128,128]{3,2,1,0:T(8,128)}, u32[]{:S(2)}, u32[]{:S(2)}) collective-permute-start(f32[2,6,128,128]{3,2,1,0:T(8,128)S(1)} %get-tuple-element.34.refs_4_), channel_id=1, source_target_pairs={{4,12},{8,0},{12,20},{16,8},{20,28},{24,16},{28,36},{32,24},{36,44... | collective-permute-start | bytes 2359304 | tf_op jit(solution)/shard_map/ppermute | solution.py:200
  44.6 1.3 %select_reduce_fusion = s32[8,3,12]{0,2,1:T(8,128)} fusion(s32[40,12]{0,1:T(8,128)S(1)} %constant_dynamic-slice_fusion, pred[8,3,40]{2,0,1:T(8,128)(4,1)S(1)} %iota_compare_fusion), kind=kLoop, calls=%fused_computation | loop fusion | flops 22752 | bytes 4032 | tf_op jit(solution)/shard_map/reduce_sum | solution.py:175
  45.9 0.8 copy.10
  46.7 1.9 %collective-permute-start.6 = (f32[2,6,128,128]{3,2,1,0:T(8,128)S(1)}, f32[2,6,128,128]{3,2,1,0:T(8,128)}, u32[]{:S(2)}, u32[]{:S(2)}) collective-permute-start(f32[2,6,128,128]{3,2,1,0:T(8,128)S(1)} %collective-permute-done.4.refs_6_), channel_id=1, source_target_pairs={{0,4},{4,0},{8,12},{12,8},{16,20},{20,16},{24,28},{28,24},{32,36},... | collective-permute-start | bytes 2359304 | tf_op jit(solution)/shard_map/ppermute | solution.py:200
  48.7 1.2 %select_reduce_fusion.1 = s32[8,3,8]{2,1,0:T(4,128)S(1)} fusion(s32[12]{0:T(128)S(1)} %iota_add_fusion, s32[8,8]{1,0:T(8,128)} %param.5, s32[8,3,12]{2,1,0:T(4,128)S(1)} %copy.10), kind=kLoop, calls=%fused_computation.1 | loop fusion | flops 6720 | bytes 2224 | tf_op jit(solution)/shard_map/reduce_sum | solution.py:178
  50.5 2.4 %collective-permute-start.10 = (f32[2,6,128,128]{3,2,1,0:T(8,128)S(1)}, f32[2,6,128,128]{3,2,1,0:T(8,128)}, u32[]{:S(2)}, u32[]{:S(2)}) collective-permute-start(f32[2,6,128,128]{3,2,1,0:T(8,128)S(1)} %get-tuple-element.34.refs_4_), channel_id=1, source_target_pairs={{0,4},{4,0},{8,12},{12,8},{16,20},{20,16},{24,28},{28,24},{32,36},... | collective-permute-start | bytes 2359304 | tf_op jit(solution)/shard_map/ppermute | solution.py:200
  53.0 1.9 %collective-permute-start.12 = (f32[2,6,128,128]{3,2,1,0:T(8,128)S(1)}, f32[2,6,128,128]{3,2,1,0:T(8,128)}, u32[]{:S(2)}, u32[]{:S(2)}) collective-permute-start(f32[2,6,128,128]{3,2,1,0:T(8,128)S(1)} %get-tuple-element.34.refs_4_), channel_id=1, source_target_pairs={{0,8},{8,16},{12,4},{16,24},{20,12},{24,32},{28,20},{32,40},{36,28... | collective-permute-start | bytes 2359304 | tf_op jit(solution)/shard_map/ppermute | solution.py:200
  54.9 1.9 %collective-permute-start.13 = (f32[2,6,128,128]{3,2,1,0:T(8,128)}, f32[2,6,128,128]{3,2,1,0:T(8,128)}, u32[]{:S(2)}, u32[]{:S(2)}) collective-permute-start(f32[2,6,128,128]{3,2,1,0:T(8,128)} %collective-permute-done.11.refs_6_), channel_id=1, source_target_pairs={{0,4},{4,0},{8,12},{12,8},{16,20},{20,16},{24,28},{28,24},{32,36},... | collective-permute-start | bytes 2359304 | tf_op jit(solution)/shard_map/ppermute | solution.py:200
  57.5 1.3 %copy.11 = s32[8,3]{1,0:T(8,128)} copy(s32[8,3]{0,1:T(4,128)} %get-tuple-element.39) | data formatting | bytes 192 | tf_op jit(solution)/shard_map/mul | solution.py:183
  61.7 6.1 %product.2 = (f32[2,4,128,128]{3,2,1,0:T(8,128)S(1)}, f32[2,4,128,128]{3,2,1,0:T(8,128)S(1)}, f32[2,4,128,128]{3,2,1,0:T(8,128)S(1)}, f32[2,4,128,128]{3,2,1,0:T(8,128)S(1)}) custom-call(s32[192]{0:T(256)S(1)} %fusion.7.where, s32[1]{0:T(128)} %bitcast.layer, f32[2,3,128,128]{3,2,1,0:T(8,128)S(1)} %get-tuple-element.22.refs_0_, ...), custom_call_target="tpu_custom_call" | custom-call | flops 2400000000 | bytes 8388608 | tf_op jit(solution)/shard_map/product/pallas_call | solution.py:125
  67.9 1.9 %collective-permute-start.7 = (f32[2,4,128,128]{3,2,1,0:T(8,128)S(1)}, f32[2,4,128,128]{3,2,1,0:T(8,128)S(1)}, u32[]{:S(2)}, u32[]{:S(2)}) collective-permute-start(f32[2,4,128,128]{3,2,1,0:T(8,128)S(1)} %get-tuple-element.31), channel_id=1, source_target_pairs={{0,1},{1,2},{2,3},{3,0},{4,5},{5,6},{6,7},{7,4},{8,9},{9,10},{10,1... | collective-permute-start | bytes 1572872 | tf_op jit(solution)/shard_map/ppermute | solution.py:212
  69.8 4.2 %collective-permute-start.8 = (f32[2,4,128,128]{3,2,1,0:T(8,128)S(1)}, f32[2,4,128,128]{3,2,1,0:T(8,128)S(1)}, u32[]{:S(2)}, u32[]{:S(2)}) collective-permute-start(f32[2,4,128,128]{3,2,1,0:T(8,128)S(1)} %get-tuple-element.32), channel_id=1, source_target_pairs={{0,2},{1,3},{2,0},{3,1},{4,6},{5,7},{6,4},{7,5},{8,10},{9,11},{10,... | collective-permute-start | bytes 1572872 | tf_op jit(solution)/shard_map/ppermute | solution.py:212
  74.0 3.1 %collective-permute-start.9 = (f32[2,4,128,128]{3,2,1,0:T(8,128)S(1)}, f32[2,4,128,128]{3,2,1,0:T(8,128)S(1)}, u32[]{:S(2)}, u32[]{:S(2)}) collective-permute-start(f32[2,4,128,128]{3,2,1,0:T(8,128)S(1)} %get-tuple-element.33), channel_id=1, source_target_pairs={{0,3},{1,0},{2,1},{3,2},{4,7},{5,4},{6,5},{7,6},{8,11},{9,8},{10,9... | collective-permute-start | bytes 1572872 | tf_op jit(solution)/shard_map/ppermute | solution.py:212
  77.1 6.6 %product.3 = (f32[2,4,128,128]{3,2,1,0:T(8,128)S(1)}, f32[2,4,128,128]{3,2,1,0:T(8,128)S(1)}, f32[2,4,128,128]{3,2,1,0:T(8,128)S(1)}, f32[2,4,128,128]{3,2,1,0:T(8,128)S(1)}) custom-call(s32[192]{0:T(256)S(1)} %fusion.7.where, s32[1]{0:T(128)} %bitcast.layer, f32[2,3,128,128]{3,2,1,0:T(8,128)S(1)} %get-tuple-element.22.refs_0_, ...), custom_call_target="tpu_custom_call" | custom-call | flops 2400000000 | bytes 8388608 | tf_op jit(solution)/shard_map/product/pallas_call | solution.py:125
  83.7 2.8 %collective-permute-start.14 = (f32[2,4,128,128]{3,2,1,0:T(8,128)S(1)}, f32[2,4,128,128]{3,2,1,0:T(8,128)S(1)}, u32[]{:S(2)}, u32[]{:S(2)}) collective-permute-start(f32[2,4,128,128]{3,2,1,0:T(8,128)S(1)} %get-tuple-element.36), channel_id=1, source_target_pairs={{0,1},{1,2},{2,3},{3,0},{4,5},{5,6},{6,7},{7,4},{8,9},{9,10},{10,1... | collective-permute-start | bytes 1572872 | tf_op jit(solution)/shard_map/ppermute | solution.py:212
  86.5 3.8 %collective-permute-start.15 = (f32[2,4,128,128]{3,2,1,0:T(8,128)S(1)}, f32[2,4,128,128]{3,2,1,0:T(8,128)S(1)}, u32[]{:S(2)}, u32[]{:S(2)}) collective-permute-start(f32[2,4,128,128]{3,2,1,0:T(8,128)S(1)} %get-tuple-element.37), channel_id=1, source_target_pairs={{0,2},{1,3},{2,0},{3,1},{4,6},{5,7},{6,4},{7,5},{8,10},{9,11},{10,... | collective-permute-start | bytes 1572872 | tf_op jit(solution)/shard_map/ppermute | solution.py:212
  90.2 6.7 %collective-permute-done.7.refs_1_ = f32[2,4,128,128]{3,2,1,0:T(8,128)S(1)} collective-permute-done((f32[2,4,128,128]{3,2,1,0:T(8,128)S(1)}, f32[2,4,128,128]{3,2,1,0:T(8,128)S(1)}, u32[]{:S(2)}, u32[]{:S(2)}) %collective-permute-start.7) | collective-permute-done | bytes 524320 | tf_op jit(solution)/shard_map/ppermute | solution.py:212
  96.9 1.9 %collective-permute-start.16 = (f32[2,4,128,128]{3,2,1,0:T(8,128)S(1)}, f32[2,4,128,128]{3,2,1,0:T(8,128)S(1)}, u32[]{:S(2)}, u32[]{:S(2)}) collective-permute-start(f32[2,4,128,128]{3,2,1,0:T(8,128)S(1)} %get-tuple-element.38), channel_id=1, source_target_pairs={{0,3},{1,0},{2,1},{3,2},{4,7},{5,4},{6,5},{7,6},{8,11},{9,8},{10,9... | collective-permute-start | bytes 1572872 | tf_op jit(solution)/shard_map/ppermute | solution.py:212
  98.8 0.9 collective-permute-done.9.refs_3_
  99.8 19.2 %collective-permute-done.14.refs_5_ = f32[2,4,128,128]{3,2,1,0:T(8,128)S(1)} collective-permute-done((f32[2,4,128,128]{3,2,1,0:T(8,128)S(1)}, f32[2,4,128,128]{3,2,1,0:T(8,128)S(1)}, u32[]{:S(2)}, u32[]{:S(2)}) %collective-permute-start.14) | collective-permute-done | bytes 524320 | tf_op jit(solution)/shard_map/ppermute | solution.py:212
  119.0 2.6 %collective-permute-done.16.refs_7_ = f32[2,4,128,128]{3,2,1,0:T(8,128)S(1)} collective-permute-done((f32[2,4,128,128]{3,2,1,0:T(8,128)S(1)}, f32[2,4,128,128]{3,2,1,0:T(8,128)S(1)}, u32[]{:S(2)}, u32[]{:S(2)}) %collective-permute-start.16) | collective-permute-done | bytes 524320 | tf_op jit(solution)/shard_map/ppermute | solution.py:212
  121.6 1.2 add_up.1
  (26 shorter events, 5.8 us)
Async XLA Ops:
  0.0 1.4 %copy-start = (f32[2,1,12,128,128]{4,3,2,1,0:T(8,128)S(1)}, f32[2,1,12,128,128]{4,3,2,1,0:T(8,128)}, u32[]{:S(2)}) copy-start(f32[2,1,12,128,128]{4,3,2,1,0:T(8,128)} %param.3) | copy-start | bytes 4718596
  2.7 0.8 copy-start.1
  3.4 28.0 %collective-permute-start.4 = (f32[2,6,128,128]{3,2,1,0:T(8,128)S(1)}, f32[2,6,128,128]{3,2,1,0:T(8,128)S(1)}, u32[]{:S(2)}, u32[]{:S(2)}) collective-permute-start(f32[2,6,128,128]{3,2,1,0:T(8,128)S(1)} %get-tuple-element.26.refs_4_), channel_id=1, source_target_pairs={{4,12},{8,0},{12,20},{16,8},{20,28},{24,16},{28,36},{32,24},{36,44... | collective-permute-start | bytes 2359304 | tf_op jit(solution)/shard_map/ppermute | solution.py:200
  14.3 21.8 %collective-permute-start.5 = (f32[2,6,128,128]{3,2,1,0:T(8,128)S(1)}, f32[2,6,128,128]{3,2,1,0:T(8,128)S(1)}, u32[]{:S(2)}, u32[]{:S(2)}) collective-permute-start(f32[2,6,128,128]{3,2,1,0:T(8,128)S(1)} %get-tuple-element.26.refs_4_), channel_id=1, source_target_pairs={{0,8},{8,16},{12,4},{16,24},{20,12},{24,32},{28,20},{32,40},{36,28... | collective-permute-start | bytes 2359304 | tf_op jit(solution)/shard_map/ppermute | solution.py:200
  16.2 45.5 %collective-permute-start.3 = (f32[2,6,128,128]{3,2,1,0:T(8,128)S(1)}, f32[2,6,128,128]{3,2,1,0:T(8,128)}, u32[]{:S(2)}, u32[]{:S(2)}) collective-permute-start(f32[2,6,128,128]{3,2,1,0:T(8,128)S(1)} %get-tuple-element.26.refs_4_), channel_id=1, source_target_pairs={{0,4},{4,0},{8,12},{12,8},{16,20},{20,16},{24,28},{28,24},{32,36},... | collective-permute-start | bytes 2359304 | tf_op jit(solution)/shard_map/ppermute | solution.py:200
  18.1 28.6 %collective-permute-start = (f32[2,3,128,128]{3,2,1,0:T(8,128)}, f32[2,3,128,128]{3,2,1,0:T(8,128)}, u32[]{:S(2)}, u32[]{:S(2)}) collective-permute-start(f32[2,3,128,128]{3,2,1,0:T(8,128)} %get-tuple-element.23), channel_id=1, source_target_pairs={{0,1},{1,2},{2,3},{3,0},{4,5},{5,6},{6,7},{7,4},{8,9},{9,10},{10,1... | collective-permute-start | bytes 1179656 | tf_op jit(solution)/shard_map/ppermute | solution.py:212
  21.5 29.0 %collective-permute-start.1 = (f32[2,3,128,128]{3,2,1,0:T(8,128)}, f32[2,3,128,128]{3,2,1,0:T(8,128)}, u32[]{:S(2)}, u32[]{:S(2)}) collective-permute-start(f32[2,3,128,128]{3,2,1,0:T(8,128)} %get-tuple-element.24), channel_id=1, source_target_pairs={{0,2},{1,3},{2,0},{3,1},{4,6},{5,7},{6,4},{7,5},{8,10},{9,11},{10,... | collective-permute-start | bytes 1179656 | tf_op jit(solution)/shard_map/ppermute | solution.py:212
  31.4 21.5 %collective-permute-start.2 = (f32[2,3,128,128]{3,2,1,0:T(8,128)}, f32[2,3,128,128]{3,2,1,0:T(8,128)}, u32[]{:S(2)}, u32[]{:S(2)}) collective-permute-start(f32[2,3,128,128]{3,2,1,0:T(8,128)} %copy-done.1), channel_id=1, source_target_pairs={{0,3},{1,0},{2,1},{3,2},{4,7},{5,4},{6,5},{7,6},{8,11},{9,8},{10,9... | collective-permute-start | bytes 1179656 | tf_op jit(solution)/shard_map/ppermute | solution.py:212
  36.1 18.8 %collective-permute-start.11 = (f32[2,6,128,128]{3,2,1,0:T(8,128)S(1)}, f32[2,6,128,128]{3,2,1,0:T(8,128)}, u32[]{:S(2)}, u32[]{:S(2)}) collective-permute-start(f32[2,6,128,128]{3,2,1,0:T(8,128)S(1)} %get-tuple-element.34.refs_4_), channel_id=1, source_target_pairs={{4,12},{8,0},{12,20},{16,8},{20,28},{24,16},{28,36},{32,24},{36,44... | collective-permute-start | bytes 2359304 | tf_op jit(solution)/shard_map/ppermute | solution.py:200
  46.7 15.0 %collective-permute-start.6 = (f32[2,6,128,128]{3,2,1,0:T(8,128)S(1)}, f32[2,6,128,128]{3,2,1,0:T(8,128)}, u32[]{:S(2)}, u32[]{:S(2)}) collective-permute-start(f32[2,6,128,128]{3,2,1,0:T(8,128)S(1)} %collective-permute-done.4.refs_6_), channel_id=1, source_target_pairs={{0,4},{4,0},{8,12},{12,8},{16,20},{20,16},{24,28},{28,24},{32,36},... | collective-permute-start | bytes 2359304 | tf_op jit(solution)/shard_map/ppermute | solution.py:200
  50.5 23.4 %collective-permute-start.10 = (f32[2,6,128,128]{3,2,1,0:T(8,128)S(1)}, f32[2,6,128,128]{3,2,1,0:T(8,128)}, u32[]{:S(2)}, u32[]{:S(2)}) collective-permute-start(f32[2,6,128,128]{3,2,1,0:T(8,128)S(1)} %get-tuple-element.34.refs_4_), channel_id=1, source_target_pairs={{0,4},{4,0},{8,12},{12,8},{16,20},{20,16},{24,28},{28,24},{32,36},... | collective-permute-start | bytes 2359304 | tf_op jit(solution)/shard_map/ppermute | solution.py:200
  53.0 24.1 %collective-permute-start.12 = (f32[2,6,128,128]{3,2,1,0:T(8,128)S(1)}, f32[2,6,128,128]{3,2,1,0:T(8,128)}, u32[]{:S(2)}, u32[]{:S(2)}) collective-permute-start(f32[2,6,128,128]{3,2,1,0:T(8,128)S(1)} %get-tuple-element.34.refs_4_), channel_id=1, source_target_pairs={{0,8},{8,16},{12,4},{16,24},{20,12},{24,32},{28,20},{32,40},{36,28... | collective-permute-start | bytes 2359304 | tf_op jit(solution)/shard_map/ppermute | solution.py:200
  54.9 22.2 %collective-permute-start.13 = (f32[2,6,128,128]{3,2,1,0:T(8,128)}, f32[2,6,128,128]{3,2,1,0:T(8,128)}, u32[]{:S(2)}, u32[]{:S(2)}) collective-permute-start(f32[2,6,128,128]{3,2,1,0:T(8,128)} %collective-permute-done.11.refs_6_), channel_id=1, source_target_pairs={{0,4},{4,0},{8,12},{12,8},{16,20},{20,16},{24,28},{28,24},{32,36},... | collective-permute-start | bytes 2359304 | tf_op jit(solution)/shard_map/ppermute | solution.py:200
  67.9 29.1 %collective-permute-start.7 = (f32[2,4,128,128]{3,2,1,0:T(8,128)S(1)}, f32[2,4,128,128]{3,2,1,0:T(8,128)S(1)}, u32[]{:S(2)}, u32[]{:S(2)}) collective-permute-start(f32[2,4,128,128]{3,2,1,0:T(8,128)S(1)} %get-tuple-element.31), channel_id=1, source_target_pairs={{0,1},{1,2},{2,3},{3,0},{4,5},{5,6},{6,7},{7,4},{8,9},{9,10},{10,1... | collective-permute-start | bytes 1572872 | tf_op jit(solution)/shard_map/ppermute | solution.py:212
  69.8 29.1 %collective-permute-start.8 = (f32[2,4,128,128]{3,2,1,0:T(8,128)S(1)}, f32[2,4,128,128]{3,2,1,0:T(8,128)S(1)}, u32[]{:S(2)}, u32[]{:S(2)}) collective-permute-start(f32[2,4,128,128]{3,2,1,0:T(8,128)S(1)} %get-tuple-element.32), channel_id=1, source_target_pairs={{0,2},{1,3},{2,0},{3,1},{4,6},{5,7},{6,4},{7,5},{8,10},{9,11},{10,... | collective-permute-start | bytes 1572872 | tf_op jit(solution)/shard_map/ppermute | solution.py:212
  74.0 25.8 %collective-permute-start.9 = (f32[2,4,128,128]{3,2,1,0:T(8,128)S(1)}, f32[2,4,128,128]{3,2,1,0:T(8,128)S(1)}, u32[]{:S(2)}, u32[]{:S(2)}) collective-permute-start(f32[2,4,128,128]{3,2,1,0:T(8,128)S(1)} %get-tuple-element.33), channel_id=1, source_target_pairs={{0,3},{1,0},{2,1},{3,2},{4,7},{5,4},{6,5},{7,6},{8,11},{9,8},{10,9... | collective-permute-start | bytes 1572872 | tf_op jit(solution)/shard_map/ppermute | solution.py:212
  83.7 35.3 %collective-permute-start.14 = (f32[2,4,128,128]{3,2,1,0:T(8,128)S(1)}, f32[2,4,128,128]{3,2,1,0:T(8,128)S(1)}, u32[]{:S(2)}, u32[]{:S(2)}) collective-permute-start(f32[2,4,128,128]{3,2,1,0:T(8,128)S(1)} %get-tuple-element.36), channel_id=1, source_target_pairs={{0,1},{1,2},{2,3},{3,0},{4,5},{5,6},{6,7},{7,4},{8,9},{9,10},{10,1... | collective-permute-start | bytes 1572872 | tf_op jit(solution)/shard_map/ppermute | solution.py:212
  86.5 32.5 %collective-permute-start.15 = (f32[2,4,128,128]{3,2,1,0:T(8,128)S(1)}, f32[2,4,128,128]{3,2,1,0:T(8,128)S(1)}, u32[]{:S(2)}, u32[]{:S(2)}) collective-permute-start(f32[2,4,128,128]{3,2,1,0:T(8,128)S(1)} %get-tuple-element.37), channel_id=1, source_target_pairs={{0,2},{1,3},{2,0},{3,1},{4,6},{5,7},{6,4},{7,5},{8,10},{9,11},{10,... | collective-permute-start | bytes 1572872 | tf_op jit(solution)/shard_map/ppermute | solution.py:212
  96.9 24.7 %collective-permute-start.16 = (f32[2,4,128,128]{3,2,1,0:T(8,128)S(1)}, f32[2,4,128,128]{3,2,1,0:T(8,128)S(1)}, u32[]{:S(2)}, u32[]{:S(2)}) collective-permute-start(f32[2,4,128,128]{3,2,1,0:T(8,128)S(1)} %get-tuple-element.38), channel_id=1, source_target_pairs={{0,3},{1,0},{2,1},{3,2},{4,7},{5,4},{6,5},{7,6},{8,11},{9,8},{10,9... | collective-permute-start | bytes 1572872 | tf_op jit(solution)/shard_map/ppermute | solution.py:212

commit v2 on v0

v2 whole, which is shorter than its diff:
```python
import functools

import jax
import jax.numpy as jnp
from jax import lax
from jax.experimental import pallas as pl
from jax.experimental.pallas import tpu as pltpu
from jax.sharding import PartitionSpec as P

HALF = 64
LAYERS = 4
ALL_ROWS = 1024
SEG = ("row", "col")
HBM = pl.BlockSpec(memory_space=pltpu.HBM)
VMEM = pl.BlockSpec(memory_space=pltpu.VMEM)
SMEM = pl.BlockSpec(memory_space=pltpu.SMEM)


def roll_half(x):
    return pltpu.roll(x, HALF, x.ndim - 1)


def left_lanes(size):
    return lax.broadcasted_iota(jnp.int32, (size, size), 1) < HALF


def pair(low, high, chunk, left):
    if chunk == 0:
        return jnp.where(left, low, roll_half(high))
    return jnp.where(left, roll_half(low), high)


def pair_rows(source, target, chunk):
    pairs = target.shape[0]
    left = left_lanes(source.shape[-1])
    for t in range(pairs):
        target[t] = pair(source[t], source[t + pairs], chunk, left)


def in_hbm(x):
    return pltpu.with_memory_space_constraint(x, pltpu.HBM)


def first_body(own, mine, half):
    rows, slots, _, _ = own.shape
    per_layer = slots // LAYERS
    for q in range(rows):
        for layer in range(LAYERS):
            mine[layer, q] = own[q, layer * per_layer : (layer + 1) * per_layer]
        pair_rows(own.at[q], half.at[q], 0)


def first(own):
    rows, slots, size, _ = own.shape
    mine, half = pl.pallas_call(
        first_body,
        in_specs=[VMEM],
        out_specs=[VMEM] * 2,
        out_shape=[
            jax.ShapeDtypeStruct((LAYERS, rows, slots // LAYERS, size, size), own.dtype),
            jax.ShapeDtypeStruct((rows, slots // 2, size, size), own.dtype),
        ],
        compiler_params=pltpu.CompilerParams(vmem_limit_bytes=12 << 20),
        cost_estimate=pl.CostEstimate(flops=0, transcendentals=0, bytes_accessed=3 << 20),
        name="first",
    )(own)
    return in_hbm(mine), in_hbm(half)


def later_body(own, other, other0, both1):
    for q in range(own.shape[0]):
        pair_rows(other.at[q], other0.at[q], 0)
        pair_rows(own.at[q], both1.at[0, q], 1)
        pair_rows(other.at[q], both1.at[1, q], 1)


def later(own, other):
    rows, slots, size, _ = own.shape
    half = (rows, slots // 2, size, size)
    return pl.pallas_call(
        later_body,
        in_specs=[VMEM] * 2,
        out_specs=[VMEM] * 2,
        out_shape=[jax.ShapeDtypeStruct(half, own.dtype), jax.ShapeDtypeStruct((2,) + half, own.dtype)],
        compiler_params=pltpu.CompilerParams(vmem_limit_bytes=12 << 20),
        cost_estimate=pl.CostEstimate(flops=0, transcendentals=0, bytes_accessed=5 << 20),
        name="later",
    )(own, other)


def second_body(both, out):
    out[...] = both[1]


def second(both):
    return pl.pallas_call(
        second_body,
        in_specs=[VMEM],
        out_specs=VMEM,
        out_shape=jax.ShapeDtypeStruct(both.shape[1:], both.dtype),
        compiler_params=pltpu.CompilerParams(vmem_limit_bytes=4 << 20),
        cost_estimate=pl.CostEstimate(flops=0, transcendentals=0, bytes_accessed=1 << 20),
        name="second",
    )(both)


def window_begin(segment, seg_rows):
    return jnp.clip(segment * seg_rows - 2 * seg_rows, 0, ALL_ROWS - 5 * seg_rows)


def find_body(segment_ref, layer_ref, near, out_cols, where):
    seg_rows, out_count = out_cols.shape
    slots, span = near.shape
    per_layer = slots // LAYERS
    rows = seg_rows // LAYERS
    segment, layer = segment_ref[0], layer_ref[0]
    begin = window_begin(segment, seg_rows)
    none = 5 * rows * slots
    odd = lax.rem(segment, 2)
    own_at = segment * seg_rows - begin

    @pl.loop(0, seg_rows)
    def _(row):
        wanted = [out_cols[row, f] for f in range(out_count)]
        for s in range(per_layer):
            inner = near[layer * per_layer + s, own_at + row]
            offset = lax.div(inner, seg_rows) - segment
            sign = jnp.where(odd == 1, -offset, offset)
            source = jnp.where(sign < 0, 4 + sign, jnp.where(sign == 2, 4, sign))
            base = (source * rows + lax.rem(lax.div(inner, LAYERS), rows)) * slots
            for f in range(out_count):
                group = lax.rem(wanted[f], LAYERS) * per_layer
                found = jnp.int32(none)
                for i in range(per_layer):
                    t = group + i
                    if f >= out_count // 2:
                        t = jnp.where(t < slots // 2, t + slots // 2, t - slots // 2)
                    found = jnp.where(near[group + i, inner - begin] == wanted[f], base + t, found)
                where[(row * per_layer + s) * out_count + f] = found


def find(segment, layer, near, out_cols):
    seg_rows, out_count = out_cols.shape
    count = seg_rows * (near.shape[0] // LAYERS) * out_count
    return pl.pallas_call(
        find_body,
        in_specs=[SMEM] * 4,
        out_specs=SMEM,
        out_shape=jax.ShapeDtypeStruct((count,), jnp.int32),
        cost_estimate=pl.CostEstimate(flops=0, transcendentals=0, bytes_accessed=1 << 20),
        name="find",
    )(segment, layer, near, out_cols)


def split(x):
    high = x.astype(jnp.bfloat16)
    return high, (x - high.astype(jnp.float32)).astype(jnp.bfloat16)


def entries_body(parts, a_high, a_low):
    _, rows, per_layer, size, _ = parts.shape
    for d in range(LAYERS):
        for q in range(rows):
            for s in range(per_layer):
                cols = slice(s * size, (s + 1) * size)
                high, low = split(parts[d, q, s])
                a_high[q * LAYERS + d, :, cols] = high
                a_low[q * LAYERS + d, :, cols] = low


def entries(parts):
    _, rows, per_layer, size, _ = parts.shape
    out = jax.ShapeDtypeStruct((LAYERS * rows, size, per_layer * size), jnp.bfloat16)
    return pl.pallas_call(
        entries_body,
        in_specs=[VMEM],
        out_specs=[VMEM] * 2,
        out_shape=[out] * 2,
        compiler_params=pltpu.CompilerParams(vmem_limit_bytes=12 << 20),
        cost_estimate=pl.CostEstimate(flops=0, transcendentals=0, bytes_accessed=3 << 20),
        name="entries",
    )(parts)


def product_body(spread, layer, where, a_high, a_low, *refs):
    count = len(refs) - (6 + (LAYERS if spread else 1))
    sources, outs, (out_v, w_high, w_low, p_high, p_low, sem) = refs[:count], refs[count:-6], refs[-6:]
    if not spread:
        outs = [outs[0].at[m] for m in range(LAYERS)]
    windows = []
    for ref in sources:
        windows += [ref] if len(ref.shape) == 4 else [ref.at[0], ref.at[1]]
    rows, pairs, size, _ = windows[0].shape
    slots = 2 * pairs
    out_pairs = out_v.shape[2]
    per_layer = slots // LAYERS
    none = len(windows) * rows * slots
    stores = [pltpu.make_async_copy(out_v.at[m], outs[m], sem.at[m]) for m in range(LAYERS)]
    w_high[none] = jnp.zeros((size, size), jnp.bfloat16)
    w_low[none] = jnp.zeros((size, size), jnp.bfloat16)
    for b, window in enumerate(windows):
        for q in range(rows):
            for t in range(pairs):
                x = window[q, t]
                base = (b * rows + q) * slots + t
                high, low = split(x)
                w_high[base], w_low[base] = high, low
                high, low = split(roll_half(x))
                w_high[base + pairs], w_low[base + pairs] = high, low
    left = left_lanes(size)
    dot = functools.partial(jnp.dot, preferred_element_type=jnp.float32)
    for at_row in range(a_high.shape[0]):
        i = at_row % 2
        owner = at_row // 2
        to_owner = (2, 1, 3, 0)[owner] if spread else owner
        row = 2 * lax.rem(layer[0] + to_owner, LAYERS) + i if spread else at_row
        for s in range(per_layer):
            at = (row * per_layer + s) * 2 * out_pairs
            for p in range(out_pairs):
                one, two = where[at + p], where[at + out_pairs + p]
                to = (i, slice(s * size, (s + 1) * size), slice(p * size, (p + 1) * size))
                p_high[to] = jnp.where(left, w_high[one], w_high[two])
                p_low[to] = jnp.where(left, w_low[one], w_low[two])
        high = a_high[row]
        total = dot(high, p_high[i]) + (dot(high, p_low[i]) + dot(a_low[row], p_high[i]))
        for p in range(out_pairs):
            out_v[to_owner, i, p] = total[:, p * size : (p + 1) * size]
        if i == 1:
            stores[to_owner].start()
    for store in stores:
        store.wait()


def product(spread, layer, where, a_high, a_low, *windows):
    rows, pairs, size, _ = windows[-1].shape
    width = a_high.shape[2]
    out_pairs = 4
    blocks = 5 * rows * 2 * pairs + 1
    out = jax.ShapeDtypeStruct((LAYERS, 2, out_pairs, size, size), jnp.float32)
    outs = [jax.ShapeDtypeStruct(out.shape[1:], out.dtype)] * LAYERS if spread else [out]
    shares = pl.pallas_call(
        functools.partial(product_body, spread),
        in_specs=[SMEM] * 2 + [VMEM] * (2 + len(windows)),
        out_specs=[HBM] * len(outs),
        out_shape=outs,
        scratch_shapes=[pltpu.VMEM(out.shape, out.dtype)]
        + [pltpu.VMEM((blocks, size, size), jnp.bfloat16)] * 2
        + [pltpu.VMEM((2, width, out_pairs * size), jnp.bfloat16)] * 2
        + [pltpu.SemaphoreType.DMA((LAYERS,))],
        compiler_params=pltpu.CompilerParams(vmem_limit_bytes=20 << 20),
        cost_estimate=pl.CostEstimate(flops=1 << 20, transcendentals=0, bytes_accessed=1 << 16),
        name="product_spread" if spread else "product",
    )(layer, where, a_high, a_low, *windows)
    return shares if spread else [in_hbm(share) for share in shares]


def add_first_body(shares, out):
    for i in range(out.shape[0]):
        for p in range(out.shape[1]):
            out[i, p] = (shares[0, i, p] + shares[1, i, p]) + (shares[2, i, p] + shares[3, i, p])


def add_first(shares):
    return pl.pallas_call(
        add_first_body,
        in_specs=[VMEM],
        out_specs=VMEM,
        out_shape=jax.ShapeDtypeStruct(shares.shape[1:], jnp.float32),
        compiler_params=pltpu.CompilerParams(vmem_limit_bytes=8 << 20),
        cost_estimate=pl.CostEstimate(flops=0, transcendentals=0, bytes_accessed=3 << 20),
        name="add_first",
    )(shares)


def add_last_body(half0, share0, share1, share2, share3, out):
    pairs = half0.shape[1]
    left = left_lanes(out.shape[-1])
    for p in range(pairs):
        one = half0[0, p]
        two = (share0[0, p] + share1[0, p]) + (share2[0, p] + share3[0, p])
        out[0, p] = jnp.where(left, one, roll_half(two))
        out[0, p + pairs] = jnp.where(left, roll_half(one), two)


def add_last(half0, shares):
    rows, pairs, size, _ = half0.shape
    spec = pl.BlockSpec((1, pairs, size, size), lambda i: (i, 0, 0, 0))
    return pl.pallas_call(
        add_last_body,
        grid=(rows,),
        in_specs=[spec] * 5,
        out_specs=pl.BlockSpec((1, 2 * pairs, size, size), lambda i: (i, 0, 0, 0)),
        out_shape=jax.ShapeDtypeStruct((rows, 2 * pairs, size, size), jnp.float32),
        compiler_params=pltpu.CompilerParams(vmem_limit_bytes=12 << 20),
        cost_estimate=pl.CostEstimate(flops=0, transcendentals=0, bytes_accessed=4 << 20),
        name="add_last",
    )(half0, *shares)


def on_device(p_values, p_cols, out_cols):
    layer = lax.axis_index("rep")
    segment = lax.axis_index(SEG)
    segments = lax.axis_size(SEG[0]) * lax.axis_size(SEG[1])
    seg_rows = out_cols.shape[0]
    own = p_values[:, 0]
    begin = window_begin(segment, seg_rows)
    segment_ref = segment.reshape(1).astype(jnp.int32)
    layer_ref = layer.reshape(1).astype(jnp.int32)

    def on_segments(x, step):
        pairs = [(i, step(i)) for i in range(segments) if 0 <= step(i) < segments]
        return lax.ppermute(x, SEG, pairs)

    def partner(x):
        return on_segments(x, lambda i: i ^ 1)

    def inward(x):
        return on_segments(x, lambda i: i - 2 if i % 2 == 0 else i + 2)

    def outward(x):
        return on_segments(x, lambda i: i + 2 if i % 2 == 0 else i - 2)

    def exchange(x):
        return lax.all_to_all(x, "rep", 0, 0, tiled=True)

    def to_layer(x, step):
        return lax.ppermute(x, "rep", [(i, (i + step) % LAYERS) for i in range(LAYERS)])

    near = lax.dynamic_slice(p_cols.T, (0, begin), (p_cols.shape[1], 5 * seg_rows))
    where = find(segment_ref, layer_ref, near, out_cols)
    mine, half0 = first(own)
    parts = exchange(mine)
    last0 = inward(half0)
    far0 = outward(half0)
    other = partner(own)
    last0, where = lax.optimization_barrier((last0, where))
    near0 = partner(last0)
    other0, here1 = later(own, other)
    here1, last0, far0, near0, parts, where = lax.optimization_barrier(
        (here1, last0, far0, near0, parts, where)
    )
    there1 = outward(here1)
    a_high, a_low = entries(parts)
    (shares0,) = product(False, layer_ref, where, a_high, a_low, half0, other0, far0, near0, last0)
    received0 = exchange(shares0)
    last1 = partner(there1[1])
    shares1 = product(True, layer_ref, where, a_high, a_low, here1, there1, last1)
    received0, kept1 = lax.optimization_barrier((received0, shares1[0]))
    received1 = [kept1] + [None] * 3
    for step in (2, 1, 3):
        received1[step] = to_layer(shares1[step], step)
    return add_last(add_first(received0), received1)


def solution(mesh):
    in_specs = (P(("row", "col"), "rep", None, None, None), P(), P(("row", "col"), None))
    out_specs = P(("row", "col", "rep"), None, None, None)
    return jax.shard_map(
        on_device, mesh=mesh, in_specs=in_specs, out_specs=out_specs, check_vma=False
    )
```

time: 235 us -> 109 us (0.46)
  the two profiles are of different devices: /device:TPU:1 before, /device:TPU:35 now
where the time goes in v2:
time: 109 us
  starting transfers between devices  53.5 us (49%)
  waiting for transfers between devices  26.6 us (24%)
  Pallas kernels  23.3 us (21%)
  local copies, waits for them, and re-layouts  5.07 us (5%)
    ppermute x6, starting transfers between devices, on_segments(): return lax.ppermute(x, SEG, pairs)  33.4 us
    ppermute x3, waiting for transfers between devices, to_layer(): lax.ppermute(x, 'rep', [(i, (i + step) % LAYERS) for i in range(LAYERS)])  20.5 us
    pallas_call x2, Pallas kernels, product(): pl.pallas_call(functools.partial(product_body, spread), in_specs=[SMEM] *...  12.9 us
    all_to_all x2, starting transfers between devices, exchange(): return lax.all_to_all(x, 'rep', 0, 0, tiled=True)  10.3 us
    ppermute x3, starting transfers between devices, to_layer(): lax.ppermute(x, 'rep', [(i, (i + step) % LAYERS) for i in range(LAYERS)])  9.7 us
    ppermute x6, waiting for transfers between devices, on_segments(): return lax.ppermute(x, SEG, pairs)  6.1 us
    unnamed x20, local copies, waits for them, and re-layouts  4.35 us
    pallas_call x1, Pallas kernels, find(): pl.pallas_call(find_body, in_specs=[SMEM] * 4, out_specs=SMEM, out_shape=...  3.45 us
  transfers between devices with their start and end apart: 11, of which 6 were waited for; matrix products, arithmetic and copies ran while one was open for 1% of the time, Pallas kernels for 20%

profile of v2, /device:TPU:35, one launch (start us, length us, event | category | flops | bytes accessed | tf_op | source)
XLA Modules:
  0.0 108.6 jit_solution(7627969366375820675)
XLA Ops:
  0.0 2.7 %collective-permute-start = (f32[2,12,128,128]{3,2,1,0:T(8,128)}, f32[2,12,128,128]{3,2,1,0:T(8,128)S(1)}, u32[]{:S(2)}, u32[]{:S(2)}) collective-permute-start(f32[2,12,128,128]{3,2,1,0:T(8,128)} %bitcast.7), channel_id=1, source_target_pairs={{0,4},{4,0},{8,12},{12,8},{16,20},{20,16},{24,28},{28,24},{32,36},... | collective-permute-start | bytes 4718600 | tf_op jit(solution)/shard_map/ppermute | solution.py:312
  2.7 0.0 copy-start.1
  2.7 1.4 %copy-done.1 = f32[2,1,12,128,128]{4,3,2,1,0:T(8,128)S(1)} copy-done((f32[2,1,12,128,128]{4,3,2,1,0:T(8,128)S(1)}, f32[2,1,12,128,128]{4,3,2,1,0:T(8,128)}, u32[]{:S(2)}) %copy-start.1) | copy-done | bytes 1572888
  4.1 1.7 %first.1 = (f32[4,2,3,128,128]{4,3,2,1,0:T(8,128)}, f32[2,6,128,128]{3,2,1,0:T(8,128)}) custom-call(f32[2,12,128,128]{3,2,1,0:T(8,128)S(1)} %bitcast.8), custom_call_target="tpu_custom_call" | custom-call | bytes 3145728 | tf_op jit(solution)/shard_map/first/pallas_call | solution.py:55
  5.8 4.0 %collective-permute-start.1 = (f32[2,6,128,128]{3,2,1,0:T(8,128)}, f32[2,6,128,128]{3,2,1,0:T(8,128)}, u32[]{:S(2)}, u32[]{:S(2)}) collective-permute-start(f32[2,6,128,128]{3,2,1,0:T(8,128)} %get-tuple-element.26.refs_0_), channel_id=1, source_target_pairs={{4,12},{8,0},{12,20},{16,8},{20,28},{24,16},{28,36},{32,24},{36,44... | collective-permute-start | bytes 2359304 | tf_op jit(solution)/shard_map/ppermute | solution.py:312
  9.8 4.7 %all-to-all-start = ((f32[4,2,3,128,128]{4,3,2,1,0:T(8,128)}), f32[4,2,3,128,128]{4,3,2,1,0:T(8,128)}, u32[]{:S(2)}, u32[]{:S(2)}) async-start(f32[4,2,3,128,128]{4,3,2,1,0:T(8,128)} %get-tuple-element.28), calls=%async_computation | async-start | bytes 3145728 | tf_op jit(solution)/shard_map/all_to_all | solution.py:324
  14.6 8.5 %collective-permute-start.2 = (f32[2,6,128,128]{3,2,1,0:T(8,128)}, f32[2,6,128,128]{3,2,1,0:T(8,128)}, u32[]{:S(2)}, u32[]{:S(2)}) collective-permute-start(f32[2,6,128,128]{3,2,1,0:T(8,128)} %get-tuple-element.26.refs_0_), channel_id=1, source_target_pairs={{0,8},{8,16},{12,4},{16,24},{20,12},{24,32},{28,20},{32,40},{36,28... | collective-permute-start | bytes 2359304 | tf_op jit(solution)/shard_map/ppermute | solution.py:312
  23.1 0.7 dynamic-slice_bitcast_fusion.near
  23.7 3.5 %find.1.where = s32[192]{0:T(256)} custom-call(s32[1]{0:T(128)} %bitcast.2.segment_ref, s32[1]{0:T(128)} %bitcast.layer_ref.layer, s32[12,40]{1,0:T(8,128)} %dynamic-slice_bitcast_fusion.near, s32[8,8]{1,0:T(8,128)} %out_cols.1), custom_call_target="tpu_custom_call" | custom-call | bytes 1048576 | tf_op jit(solution)/shard_map/find/pallas_call | solution.py:145
  27.2 3.3 %collective-permute-start.3 = (f32[2,6,128,128]{3,2,1,0:T(8,128)}, f32[2,6,128,128]{3,2,1,0:T(8,128)}, u32[]{:S(2)}, u32[]{:S(2)}) collective-permute-start(f32[2,6,128,128]{3,2,1,0:T(8,128)} %collective-permute-done.1.refs_4_), channel_id=1, source_target_pairs={{0,4},{4,0},{8,12},{12,8},{16,20},{20,16},{24,28},{28,24},{32,36},... | collective-permute-start | bytes 2359304 | tf_op jit(solution)/shard_map/ppermute | solution.py:312
  30.6 0.7 later.1
  31.3 1.2 %copy-done.3 = f32[2,2,6,128,128]{4,3,2,1,0:T(8,128)} copy-done((f32[2,2,6,128,128]{4,3,2,1,0:T(8,128)}, f32[2,2,6,128,128]{4,3,2,1,0:T(8,128)S(1)}, u32[]{:S(2)}) %copy-start.3) | copy-done | bytes 1572888
  32.4 0.9 copy-done.5
  33.4 1.1 %collective-permute-done.2.refs_2_ = f32[2,6,128,128]{3,2,1,0:T(8,128)} collective-permute-done((f32[2,6,128,128]{3,2,1,0:T(8,128)}, f32[2,6,128,128]{3,2,1,0:T(8,128)}, u32[]{:S(2)}, u32[]{:S(2)}) %collective-permute-start.2) | collective-permute-done | bytes 786464 | tf_op jit(solution)/shard_map/ppermute | solution.py:312
  34.5 7.8 %collective-permute-start.4 = (f32[2,2,6,128,128]{4,3,2,1,0:T(8,128)}, f32[2,2,6,128,128]{4,3,2,1,0:T(8,128)S(1)}, u32[]{:S(2)}, u32[]{:S(2)}) collective-permute-start(f32[2,2,6,128,128]{4,3,2,1,0:T(8,128)} %copy-done.3), channel_id=1, source_target_pairs={{0,8},{8,16},{12,4},{16,24},{20,12},{24,32},{28,20},{32,40},{36,28... | collective-permute-start | bytes 4718600 | tf_op jit(solution)/shard_map/ppermute | solution.py:312
  42.4 1.7 %entries.1 = (bf16[8,128,384]{2,1,0:T(8,128)(2,1)S(1)}, bf16[8,128,384]{2,1,0:T(8,128)(2,1)S(1)}) custom-call(f32[4,2,3,128,128]{4,3,2,1,0:T(8,128)} %all-to-all-done.parts), custom_call_target="tpu_custom_call" | custom-call | bytes 3145728 | tf_op jit(solution)/shard_map/entries/pallas_call | solution.py:174
  44.1 7.3 %product.1 = f32[4,2,4,128,128]{4,3,2,1,0:T(8,128)} custom-call(s32[1]{0:T(128)} %bitcast.layer_ref.layer, s32[192]{0:T(256)S(1)} %copy-done.9, bf16[8,128,384]{2,1,0:T(8,128)(2,1)S(1)} %get-tuple-element.32.a_high, bf16[8,128,384]{2,1,0:T(8,128)(2,1)S(1)} %get-tuple-element.33.a_low, f32[2,6,128,128]{3,2,1,0:T(8,128)} %get-tuple-element.26.refs_0_, ...), custom_call_target="tpu_custom_call" | custom-call | flops 1048576 | bytes 65536 | tf_op jit(solution)/shard_map/product/pallas_call | solution.py:241
  51.3 5.6 %all-to-all-start.1 = ((f32[4,2,4,128,128]{4,3,2,1,0:T(8,128)}), f32[4,2,4,128,128]{4,3,2,1,0:T(8,128)}, u32[]{:S(2)}, u32[]{:S(2)}) async-start(f32[4,2,4,128,128]{4,3,2,1,0:T(8,128)} %product.1), calls=%async_computation.1 | async-start | bytes 4194304 | tf_op jit(solution)/shard_map/all_to_all | solution.py:324
  56.9 3.1 %collective-permute-done.4.refs_1_ = f32[2,2,6,128,128]{4,3,2,1,0:T(8,128)S(1)} collective-permute-done((f32[2,2,6,128,128]{4,3,2,1,0:T(8,128)}, f32[2,2,6,128,128]{4,3,2,1,0:T(8,128)S(1)}, u32[]{:S(2)}, u32[]{:S(2)}) %collective-permute-start.4) | collective-permute-done | bytes 1572896 | tf_op jit(solution)/shard_map/ppermute | solution.py:312
  60.0 0.1 slice_bitcast_fusion
  60.1 7.1 %collective-permute-start.5 = (f32[2,6,128,128]{3,2,1,0:T(8,128)S(1)}, f32[2,6,128,128]{3,2,1,0:T(8,128)S(1)}, u32[]{:S(2)}, u32[]{:S(2)}) collective-permute-start(f32[2,6,128,128]{3,2,1,0:T(8,128)S(1)} %slice_bitcast_fusion), channel_id=1, source_target_pairs={{0,4},{4,0},{8,12},{12,8},{16,20},{20,16},{24,28},{28,24},{32,36},... | collective-permute-start | bytes 2359304 | tf_op jit(solution)/shard_map/ppermute | solution.py:312
  67.2 1.9 %collective-permute-done.5.refs_2_ = f32[2,6,128,128]{3,2,1,0:T(8,128)S(1)} collective-permute-done((f32[2,6,128,128]{3,2,1,0:T(8,128)S(1)}, f32[2,6,128,128]{3,2,1,0:T(8,128)S(1)}, u32[]{:S(2)}, u32[]{:S(2)}) %collective-permute-start.5) | collective-permute-done | bytes 786464 | tf_op jit(solution)/shard_map/ppermute | solution.py:312
  69.1 5.6 %product_spread.1 = (f32[2,4,128,128]{3,2,1,0:T(8,128)S(1)}, f32[2,4,128,128]{3,2,1,0:T(8,128)}, f32[2,4,128,128]{3,2,1,0:T(8,128)}, f32[2,4,128,128]{3,2,1,0:T(8,128)}) custom-call(s32[1]{0:T(128)} %bitcast.layer_ref.layer, s32[192]{0:T(256)S(1)} %copy-done.9, bf16[8,128,384]{2,1,0:T(8,128)(2,1)S(1)} %get-tuple-element.32.a_high, ...), custom_call_target="tpu_custom_call" | custom-call | flops 1048576 | bytes 65536 | tf_op jit(solution)/shard_map/product_spread/pallas_call | solution.py:241
  74.7 0.8 copy-done.7
  75.5 3.2 %collective-permute-start.6 = (f32[2,4,128,128]{3,2,1,0:T(8,128)}, f32[2,4,128,128]{3,2,1,0:T(8,128)S(1)}, u32[]{:S(2)}, u32[]{:S(2)}) collective-permute-start(f32[2,4,128,128]{3,2,1,0:T(8,128)} %get-tuple-element.42), channel_id=1, source_target_pairs={{0,1},{1,2},{2,3},{3,0},{4,5},{5,6},{6,7},{7,4},{8,9},{9,10},{10,1... | collective-permute-start | bytes 1572872 | tf_op jit(solution)/shard_map/ppermute | solution.py:327
  78.7 2.5 %collective-permute-start.7 = (f32[2,4,128,128]{3,2,1,0:T(8,128)}, f32[2,4,128,128]{3,2,1,0:T(8,128)S(1)}, u32[]{:S(2)}, u32[]{:S(2)}) collective-permute-start(f32[2,4,128,128]{3,2,1,0:T(8,128)} %get-tuple-element.43), channel_id=1, source_target_pairs={{0,2},{1,3},{2,0},{3,1},{4,6},{5,7},{6,4},{7,5},{8,10},{9,11},{10,... | collective-permute-start | bytes 1572872 | tf_op jit(solution)/shard_map/ppermute | solution.py:327
  81.2 4.0 %collective-permute-start.8 = (f32[2,4,128,128]{3,2,1,0:T(8,128)}, f32[2,4,128,128]{3,2,1,0:T(8,128)S(1)}, u32[]{:S(2)}, u32[]{:S(2)}) collective-permute-start(f32[2,4,128,128]{3,2,1,0:T(8,128)} %get-tuple-element.44), channel_id=1, source_target_pairs={{0,3},{1,0},{2,1},{3,2},{4,7},{5,4},{6,5},{7,6},{8,11},{9,8},{10,9... | collective-permute-start | bytes 1572872 | tf_op jit(solution)/shard_map/ppermute | solution.py:327
  85.2 1.7 %add_first.1.half0 = f32[2,4,128,128]{3,2,1,0:T(8,128)S(1)} custom-call(f32[4,2,4,128,128]{4,3,2,1,0:T(8,128)} %all-to-all-done.1.shares), custom_call_target="tpu_custom_call" | custom-call | bytes 3145728 | tf_op jit(solution)/shard_map/add_first/pallas_call | solution.py:264
  86.9 3.9 %collective-permute-done.6.share1 = f32[2,4,128,128]{3,2,1,0:T(8,128)S(1)} collective-permute-done((f32[2,4,128,128]{3,2,1,0:T(8,128)}, f32[2,4,128,128]{3,2,1,0:T(8,128)S(1)}, u32[]{:S(2)}, u32[]{:S(2)}) %collective-permute-start.6) | collective-permute-done | bytes 524320 | tf_op jit(solution)/shard_map/ppermute | solution.py:327
  90.9 4.3 %collective-permute-done.7.share2 = f32[2,4,128,128]{3,2,1,0:T(8,128)S(1)} collective-permute-done((f32[2,4,128,128]{3,2,1,0:T(8,128)}, f32[2,4,128,128]{3,2,1,0:T(8,128)S(1)}, u32[]{:S(2)}, u32[]{:S(2)}) %collective-permute-start.7) | collective-permute-done | bytes 524320 | tf_op jit(solution)/shard_map/ppermute | solution.py:327
  95.2 12.2 %collective-permute-done.8.share3 = f32[2,4,128,128]{3,2,1,0:T(8,128)S(1)} collective-permute-done((f32[2,4,128,128]{3,2,1,0:T(8,128)}, f32[2,4,128,128]{3,2,1,0:T(8,128)S(1)}, u32[]{:S(2)}, u32[]{:S(2)}) %collective-permute-start.8) | collective-permute-done | bytes 524320 | tf_op jit(solution)/shard_map/ppermute | solution.py:327
  107.4 1.2 %add_last.1 = f32[2,8,128,128]{3,2,1,0:T(8,128)} custom-call(f32[2,4,128,128]{3,2,1,0:T(8,128)S(1)} %add_first.1.half0, f32[2,4,128,128]{3,2,1,0:T(8,128)S(1)} %copy-done.8, f32[2,4,128,128]{3,2,1,0:T(8,128)S(1)} %collective-permute-done.6.share1, f32[2,4,128,128]{3,2,1,0:T(8,128)S(1)} %collective-permute-done.7.share2, ...), custom_call_target="tpu_custom_call" | custom-call | bytes 4194304 | tf_op jit(solution)/shard_map/add_last/pallas_call | solution.py:288
  (20 shorter events, 0.0 us)
Async XLA Ops:
  0.0 23.1 %copy-start = (s32[1024,12]{0,1:T(8,128)S(1)}, s32[1024,12]{0,1:T(8,128)}, u32[]{:S(2)}) copy-start(s32[1024,12]{0,1:T(8,128)} %param.4) | copy-start | bytes 147460
  0.0 30.6 %collective-permute-start = (f32[2,12,128,128]{3,2,1,0:T(8,128)}, f32[2,12,128,128]{3,2,1,0:T(8,128)S(1)}, u32[]{:S(2)}, u32[]{:S(2)}) collective-permute-start(f32[2,12,128,128]{3,2,1,0:T(8,128)} %bitcast.7), channel_id=1, source_target_pairs={{0,4},{4,0},{8,12},{12,8},{16,20},{20,16},{24,28},{28,24},{32,36},... | collective-permute-start | bytes 4718600 | tf_op jit(solution)/shard_map/ppermute | solution.py:312
  2.7 1.4 %copy-start.1 = (f32[2,1,12,128,128]{4,3,2,1,0:T(8,128)S(1)}, f32[2,1,12,128,128]{4,3,2,1,0:T(8,128)}, u32[]{:S(2)}) copy-start(f32[2,1,12,128,128]{4,3,2,1,0:T(8,128)} %param.3) | copy-start | bytes 4718596
  5.8 21.4 %collective-permute-start.1 = (f32[2,6,128,128]{3,2,1,0:T(8,128)}, f32[2,6,128,128]{3,2,1,0:T(8,128)}, u32[]{:S(2)}, u32[]{:S(2)}) collective-permute-start(f32[2,6,128,128]{3,2,1,0:T(8,128)} %get-tuple-element.26.refs_0_), channel_id=1, source_target_pairs={{4,12},{8,0},{12,20},{16,8},{20,28},{24,16},{28,36},{32,24},{36,44... | collective-permute-start | bytes 2359304 | tf_op jit(solution)/shard_map/ppermute | solution.py:312
  9.8 20.7 %copy-start.2 = (f32[2,1,12,128,128]{4,3,2,1,0:T(8,128)S(1)}, f32[2,1,12,128,128]{4,3,2,1,0:T(8,128)}, u32[]{:S(2)}) copy-start(f32[2,1,12,128,128]{4,3,2,1,0:T(8,128)} %param.3) | copy-start | bytes 4718596
  9.8 24.7 %all-to-all-start = ((f32[4,2,3,128,128]{4,3,2,1,0:T(8,128)}), f32[4,2,3,128,128]{4,3,2,1,0:T(8,128)}, u32[]{:S(2)}, u32[]{:S(2)}) async-start(f32[4,2,3,128,128]{4,3,2,1,0:T(8,128)} %get-tuple-element.28), calls=%async_computation | async-start | bytes 3145728 | tf_op jit(solution)/shard_map/all_to_all | solution.py:324
  14.6 19.9 %collective-permute-start.2 = (f32[2,6,128,128]{3,2,1,0:T(8,128)}, f32[2,6,128,128]{3,2,1,0:T(8,128)}, u32[]{:S(2)}, u32[]{:S(2)}) collective-permute-start(f32[2,6,128,128]{3,2,1,0:T(8,128)} %get-tuple-element.26.refs_0_), channel_id=1, source_target_pairs={{0,8},{8,16},{12,4},{16,24},{20,12},{24,32},{28,20},{32,40},{36,28... | collective-permute-start | bytes 2359304 | tf_op jit(solution)/shard_map/ppermute | solution.py:312
  27.2 7.3 %collective-permute-start.3 = (f32[2,6,128,128]{3,2,1,0:T(8,128)}, f32[2,6,128,128]{3,2,1,0:T(8,128)}, u32[]{:S(2)}, u32[]{:S(2)}) collective-permute-start(f32[2,6,128,128]{3,2,1,0:T(8,128)} %collective-permute-done.1.refs_4_), channel_id=1, source_target_pairs={{0,4},{4,0},{8,12},{12,8},{16,20},{20,16},{24,28},{28,24},{32,36},... | collective-permute-start | bytes 2359304 | tf_op jit(solution)/shard_map/ppermute | solution.py:312
  31.3 1.2 %copy-start.3 = (f32[2,2,6,128,128]{4,3,2,1,0:T(8,128)}, f32[2,2,6,128,128]{4,3,2,1,0:T(8,128)S(1)}, u32[]{:S(2)}) copy-start(f32[2,2,6,128,128]{4,3,2,1,0:T(8,128)S(1)} %get-tuple-element.38.refs_0_) | copy-start | bytes 4718596
  32.4 0.9 copy-start.5
  33.4 10.7 %copy-start.9 = (s32[192]{0:T(256)S(1)}, s32[192]{0:T(256)}, u32[]{:S(2)}) copy-start(s32[192]{0:T(256)} %find.1.where) | copy-start | bytes 2308
  34.5 9.5 %copy-start.6 = (f32[2,6,128,128]{3,2,1,0:T(8,128)S(1)}, f32[2,6,128,128]{3,2,1,0:T(8,128)}, u32[]{:S(2)}) copy-start(f32[2,6,128,128]{3,2,1,0:T(8,128)} %copy-done.5) | copy-start | bytes 2359300
  34.5 25.5 %collective-permute-start.4 = (f32[2,2,6,128,128]{4,3,2,1,0:T(8,128)}, f32[2,2,6,128,128]{4,3,2,1,0:T(8,128)S(1)}, u32[]{:S(2)}, u32[]{:S(2)}) collective-permute-start(f32[2,2,6,128,128]{4,3,2,1,0:T(8,128)} %copy-done.3), channel_id=1, source_target_pairs={{0,8},{8,16},{12,4},{16,24},{20,12},{24,32},{28,20},{32,40},{36,28... | collective-permute-start | bytes 4718600 | tf_op jit(solution)/shard_map/ppermute | solution.py:312
  51.3 33.9 %all-to-all-start.1 = ((f32[4,2,4,128,128]{4,3,2,1,0:T(8,128)}), f32[4,2,4,128,128]{4,3,2,1,0:T(8,128)}, u32[]{:S(2)}, u32[]{:S(2)}) async-start(f32[4,2,4,128,128]{4,3,2,1,0:T(8,128)} %product.1), calls=%async_computation.1 | async-start | bytes 4194304 | tf_op jit(solution)/shard_map/all_to_all | solution.py:324
  56.9 12.1 %copy-start.4 = (f32[2,2,6,128,128]{4,3,2,1,0:T(8,128)S(1)}, f32[2,2,6,128,128]{4,3,2,1,0:T(8,128)}, u32[]{:S(2)}) copy-start(f32[2,2,6,128,128]{4,3,2,1,0:T(8,128)} %copy-done.3) | copy-start | bytes 4718596
  60.1 9.0 %collective-permute-start.5 = (f32[2,6,128,128]{3,2,1,0:T(8,128)S(1)}, f32[2,6,128,128]{3,2,1,0:T(8,128)S(1)}, u32[]{:S(2)}, u32[]{:S(2)}) collective-permute-start(f32[2,6,128,128]{3,2,1,0:T(8,128)S(1)} %slice_bitcast_fusion), channel_id=1, source_target_pairs={{0,4},{4,0},{8,12},{12,8},{16,20},{20,16},{24,28},{28,24},{32,36},... | collective-permute-start | bytes 2359304 | tf_op jit(solution)/shard_map/ppermute | solution.py:312
  74.7 0.8 copy-start.7
  75.5 31.9 %copy-start.8 = (f32[2,4,128,128]{3,2,1,0:T(8,128)S(1)}, f32[2,4,128,128]{3,2,1,0:T(8,128)}, u32[]{:S(2)}) copy-start(f32[2,4,128,128]{3,2,1,0:T(8,128)} %copy-done.7) | copy-start | bytes 1572868
  75.5 15.4 %collective-permute-start.6 = (f32[2,4,128,128]{3,2,1,0:T(8,128)}, f32[2,4,128,128]{3,2,1,0:T(8,128)S(1)}, u32[]{:S(2)}, u32[]{:S(2)}) collective-permute-start(f32[2,4,128,128]{3,2,1,0:T(8,128)} %get-tuple-element.42), channel_id=1, source_target_pairs={{0,1},{1,2},{2,3},{3,0},{4,5},{5,6},{6,7},{7,4},{8,9},{9,10},{10,1... | collective-permute-start | bytes 1572872 | tf_op jit(solution)/shard_map/ppermute | solution.py:327
  78.7 16.5 %collective-permute-start.7 = (f32[2,4,128,128]{3,2,1,0:T(8,128)}, f32[2,4,128,128]{3,2,1,0:T(8,128)S(1)}, u32[]{:S(2)}, u32[]{:S(2)}) collective-permute-start(f32[2,4,128,128]{3,2,1,0:T(8,128)} %get-tuple-element.43), channel_id=1, source_target_pairs={{0,2},{1,3},{2,0},{3,1},{4,6},{5,7},{6,4},{7,5},{8,10},{9,11},{10,... | collective-permute-start | bytes 1572872 | tf_op jit(solution)/shard_map/ppermute | solution.py:327
  81.2 26.2 %collective-permute-start.8 = (f32[2,4,128,128]{3,2,1,0:T(8,128)}, f32[2,4,128,128]{3,2,1,0:T(8,128)S(1)}, u32[]{:S(2)}, u32[]{:S(2)}) collective-permute-start(f32[2,4,128,128]{3,2,1,0:T(8,128)} %get-tuple-element.44), channel_id=1, source_target_pairs={{0,3},{1,0},{2,1},{3,2},{4,7},{5,4},{6,5},{7,6},{8,11},{9,8},{10,9... | collective-permute-start | bytes 1572872 | tf_op jit(solution)/shard_map/ppermute | solution.py:327

commit v3 on v2

v3 whole, which is shorter than its diff:
```python
import functools

import jax
import jax.numpy as jnp
from jax import lax
from jax.experimental import pallas as pl
from jax.experimental.pallas import tpu as pltpu
from jax.sharding import PartitionSpec as P

HALF = 64
LAYERS = 4
ALL_ROWS = 1024
SEG = ("row", "col")
HBM = pl.BlockSpec(memory_space=pltpu.HBM)
VMEM = pl.BlockSpec(memory_space=pltpu.VMEM)
SMEM = pl.BlockSpec(memory_space=pltpu.SMEM)


def turned(block, chunk):
    return block.T[chunk * HALF : (chunk + 1) * HALF]


def in_hbm(x):
    return pltpu.with_memory_space_constraint(x, pltpu.HBM)


def first_body(own, mine, half):
    rows, slots, _, _ = own.shape
    per_layer = slots // LAYERS
    for q in range(rows):
        for layer in range(LAYERS):
            mine[layer, q] = own[q, layer * per_layer : (layer + 1) * per_layer]
        for t in range(slots):
            half[q, t] = turned(own[q, t], 0)


def first(own):
    rows, slots, size, _ = own.shape
    mine, half = pl.pallas_call(
        first_body,
        in_specs=[VMEM],
        out_specs=[VMEM] * 2,
        out_shape=[
            jax.ShapeDtypeStruct((LAYERS, rows, slots // LAYERS, size, size), own.dtype),
            jax.ShapeDtypeStruct((rows, slots, HALF, size), own.dtype),
        ],
        compiler_params=pltpu.CompilerParams(vmem_limit_bytes=12 << 20),
        cost_estimate=pl.CostEstimate(flops=0, transcendentals=0, bytes_accessed=3 << 20),
        name="first",
    )(own)
    return in_hbm(mine), in_hbm(half)


def later_body(own, other, other0, both1):
    for q in range(own.shape[0]):
        for t in range(own.shape[1]):
            both1[0, q, t] = turned(own[q, t], 1)
            whole = other[q, t].T
            other0[q, t] = whole[:HALF]
            both1[1, q, t] = whole[HALF:]


def later(own, other):
    rows, slots, size, _ = own.shape
    half = (rows, slots, HALF, size)
    return pl.pallas_call(
        later_body,
        in_specs=[VMEM] * 2,
        out_specs=[VMEM] * 2,
        out_shape=[jax.ShapeDtypeStruct(half, own.dtype), jax.ShapeDtypeStruct((2,) + half, own.dtype)],
        compiler_params=pltpu.CompilerParams(vmem_limit_bytes=12 << 20),
        cost_estimate=pl.CostEstimate(flops=0, transcendentals=0, bytes_accessed=5 << 20),
        name="later",
    )(own, other)


def window_begin(segment, seg_rows):
    return jnp.clip(segment * seg_rows - 2 * seg_rows, 0, ALL_ROWS - 5 * seg_rows)


def find_body(segment_ref, layer_ref, near, out_cols, where):
    seg_rows, out_count = out_cols.shape
    slots, span = near.shape
    per_layer = slots // LAYERS
    rows = seg_rows // LAYERS
    segment, layer = segment_ref[0], layer_ref[0]
    begin = window_begin(segment, seg_rows)
    none = 5 * rows * slots
    odd = lax.rem(segment, 2)
    own_at = segment * seg_rows - begin

    @pl.loop(0, seg_rows)
    def _(row):
        wanted = [out_cols[row, f] for f in range(out_count)]
        for s in range(per_layer):
            inner = near[layer * per_layer + s, own_at + row]
            offset = lax.div(inner, seg_rows) - segment
            sign = jnp.where(odd == 1, -offset, offset)
            source = jnp.where(sign < 0, 4 + sign, jnp.where(sign == 2, 4, sign))
            base = (source * rows + lax.rem(lax.div(inner, LAYERS), rows)) * slots
            for f in range(out_count):
                group = lax.rem(wanted[f], LAYERS) * per_layer
                found = jnp.int32(none)
                for i in range(per_layer):
                    t = group + i
                    found = jnp.where(near[group + i, inner - begin] == wanted[f], base + t, found)
                where[(row * per_layer + s) * out_count + f] = found


def find(segment, layer, near, out_cols):
    seg_rows, out_count = out_cols.shape
    count = seg_rows * (near.shape[0] // LAYERS) * out_count
    return pl.pallas_call(
        find_body,
        in_specs=[SMEM] * 4,
        out_specs=SMEM,
        out_shape=jax.ShapeDtypeStruct((count,), jnp.int32),
        cost_estimate=pl.CostEstimate(flops=0, transcendentals=0, bytes_accessed=1 << 20),
        name="find",
    )(segment, layer, near, out_cols)


def split(x):
    high = x.astype(jnp.bfloat16)
    return high, (x - high.astype(jnp.float32)).astype(jnp.bfloat16)


def split_entries(parts, entry):
    _, rows, per_layer, size, _ = parts.shape
    for d in range(LAYERS):
        for q in range(rows):
            for s in range(per_layer):
                cols = slice(s * size, (s + 1) * size)
                high, low = split(parts[d, q, s])
                entry[q * LAYERS + d, :size, cols] = high
                entry[q * LAYERS + d, size:, cols] = low


def product_body(spread, layer, where, parts, *refs):
    count = len(refs) - (7 + (LAYERS if spread else 1))
    sources, outs, (out_v, entry, w_high, w_low, p_high, p_low, sem) = refs[:count], refs[count:-7], refs[-7:]
    if not spread:
        outs = [outs[0].at[m] for m in range(LAYERS)]
    windows = []
    for ref in sources:
        windows += [ref] if len(ref.shape) == 4 else [ref.at[0], ref.at[1]]
    rows, slots, _, size = windows[0].shape
    out_count = out_v.shape[2]
    per_layer = slots // LAYERS
    none = len(windows) * rows * slots
    stores = [pltpu.make_async_copy(out_v.at[m], outs[m], sem.at[m]) for m in range(LAYERS)]
    split_entries(parts, entry)
    w_high[none] = jnp.zeros((HALF, size), jnp.bfloat16)
    w_low[none] = jnp.zeros((HALF, size), jnp.bfloat16)
    for b, window in enumerate(windows):
        for q in range(rows):
            for t in range(slots):
                at = (b * rows + q) * slots + t
                w_high[at], w_low[at] = split(window[q, t])

    def dot(x, y):
        return lax.dot_general(x, y, (((1,), (1,)), ((), ())), preferred_element_type=jnp.float32)

    for at_row in range(entry.shape[0]):
        i = at_row % 2
        owner = at_row // 2
        to_owner = (2, 1, 3, 0)[owner] if spread else owner
        row = 2 * lax.rem(layer[0] + to_owner, LAYERS) + i if spread else at_row
        for s in range(per_layer):
            at = (row * per_layer + s) * out_count
            for f in range(out_count):
                found = where[at + f]
                to = (i, slice(f * HALF, (f + 1) * HALF), slice(s * size, (s + 1) * size))
                p_high[to] = w_high[found]
                p_low[to] = w_low[found]
        wide = dot(p_high[i], entry[row])
        total = wide[:, :size] + (wide[:, size:] + dot(p_low[i], entry[row, :size]))
        out_v[to_owner, i] = total.reshape(out_count, HALF, size)
        if i == 1:
            stores[to_owner].start()
    for store in stores:
        store.wait()


def product(spread, layer, where, parts, *windows):
    rows, slots, _, size = windows[-1].shape
    width = parts.shape[2] * size
    out_count = 8
    blocks = 5 * rows * slots + 1
    out = jax.ShapeDtypeStruct((LAYERS, 2, out_count, HALF, size), jnp.float32)
    outs = [jax.ShapeDtypeStruct(out.shape[1:], out.dtype)] * LAYERS if spread else [out]
    shares = pl.pallas_call(
        functools.partial(product_body, spread),
        in_specs=[SMEM] * 2 + [VMEM] * (1 + len(windows)),
        out_specs=[HBM] * len(outs),
        out_shape=outs,
        scratch_shapes=[
            pltpu.VMEM(out.shape, out.dtype),
            pltpu.VMEM((LAYERS * rows, 2 * size, width), jnp.bfloat16),
        ]
        + [pltpu.VMEM((blocks, HALF, size), jnp.bfloat16)] * 2
        + [pltpu.VMEM((2, out_count * HALF, width), jnp.bfloat16)] * 2
        + [pltpu.SemaphoreType.DMA((LAYERS,))],
        compiler_params=pltpu.CompilerParams(vmem_limit_bytes=(20 if spread else 60) << 20),
        cost_estimate=pl.CostEstimate(flops=1 << 20, transcendentals=0, bytes_accessed=1 << 16),
        name="product_spread" if spread else "product",
    )(layer, where, parts, *windows)
    return shares if spread else [in_hbm(share) for share in shares]


def add_first_body(shares, out):
    for i in range(out.shape[0]):
        for p in range(out.shape[1]):
            out[i, p] = (shares[0, i, p] + shares[1, i, p]) + (shares[2, i, p] + shares[3, i, p])


def add_first(shares):
    return pl.pallas_call(
        add_first_body,
        in_specs=[VMEM],
        out_specs=VMEM,
        out_shape=jax.ShapeDtypeStruct(shares.shape[1:], jnp.float32),
        compiler_params=pltpu.CompilerParams(vmem_limit_bytes=8 << 20),
        cost_estimate=pl.CostEstimate(flops=0, transcendentals=0, bytes_accessed=3 << 20),
        name="add_first",
    )(shares)


def add_last_body(half0, share0, share1, share2, share3, out):
    for f in range(half0.shape[1]):
        two = (share0[0, f] + share1[0, f]) + (share2[0, f] + share3[0, f])
        out[0, f] = jnp.concatenate([half0[0, f], two], axis=0).T


def add_last(half0, shares):
    rows, count, _, size = half0.shape
    spec = pl.BlockSpec((1, count, HALF, size), lambda i: (i, 0, 0, 0))
    return pl.pallas_call(
        add_last_body,
        grid=(rows,),
        in_specs=[spec] * 5,
        out_specs=pl.BlockSpec((1, count, size, size), lambda i: (i, 0, 0, 0)),
        out_shape=jax.ShapeDtypeStruct((rows, count, size, size), jnp.float32),
        compiler_params=pltpu.CompilerParams(vmem_limit_bytes=12 << 20),
        cost_estimate=pl.CostEstimate(flops=0, transcendentals=0, bytes_accessed=4 << 20),
        name="add_last",
    )(half0, *shares)


def on_device(p_values, p_cols, out_cols):
    layer = lax.axis_index("rep")
    segment = lax.axis_index(SEG)
    segments = lax.axis_size(SEG[0]) * lax.axis_size(SEG[1])
    seg_rows = out_cols.shape[0]
    own = p_values[:, 0]
    begin = window_begin(segment, seg_rows)
    segment_ref = segment.reshape(1).astype(jnp.int32)
    layer_ref = layer.reshape(1).astype(jnp.int32)

    def on_segments(x, step):
        pairs = [(i, step(i)) for i in range(segments) if 0 <= step(i) < segments]
        return lax.ppermute(x, SEG, pairs)

    def partner(x):
        return on_segments(x, lambda i: i ^ 1)

    def inward(x):
        return on_segments(x, lambda i: i - 2 if i % 2 == 0 else i + 2)

    def outward(x):
        return on_segments(x, lambda i: i + 2 if i % 2 == 0 else i - 2)

    def exchange(x):
        return lax.all_to_all(x, "rep", 0, 0, tiled=True)

    def to_layer(x, step):
        return lax.ppermute(x, "rep", [(i, (i + step) % LAYERS) for i in range(LAYERS)])

    near = lax.dynamic_slice(p_cols.T, (0, begin), (p_cols.shape[1], 5 * seg_rows))
    where = find(segment_ref, layer_ref, near, out_cols)
    mine, half0 = first(own)
    parts = exchange(mine)
    last0 = inward(half0)
    far0 = outward(half0)
    other = partner(own)
    last0, where = lax.optimization_barrier((last0, where))
    near0 = partner(last0)
    other0, here1 = later(own, other)
    here1, last0, far0, near0, parts, where = lax.optimization_barrier(
        (here1, last0, far0, near0, parts, where)
    )
    there1 = outward(here1)
    (shares0,) = product(False, layer_ref, where, parts, half0, other0, far0, near0, last0)
    received0 = exchange(shares0)
    last1 = partner(there1[1])
    shares1 = product(True, layer_ref, where, parts, here1, there1, last1)
    received0, kept1 = lax.optimization_barrier((received0, shares1[0]))
    received1 = [kept1] + [None] * 3
    for step in (2, 1, 3):
        received1[step] = to_layer(shares1[step], step)
    return add_last(add_first(received0), received1)


def solution(mesh):
    in_specs = (P(("row", "col"), "rep", None, None, None), P(), P(("row", "col"), None))
    out_specs = P(("row", "col", "rep"), None, None, None)
    return jax.shard_map(
        on_device, mesh=mesh, in_specs=in_specs, out_specs=out_specs, check_vma=False
    )
```

time: 109 us -> 108 us (level)
  Pallas kernels: 23.3 us -> 20.6 us
  waiting for transfers between devices: 26.6 us -> 28.4 us
    ppermute x6, waiting for transfers between devices: 6.1 us -> 8.16 us  [on_segments(): return lax.ppermute(x, SEG, pairs)]
    pallas_call x1 -> x0, Pallas kernels: 1.67 us -> none  [entries(): pl.pallas_call(entries_body, in_specs=[VMEM], out_specs=[VMEM] * 2, out_s...]
    pallas_call x2, Pallas kernels: 12.9 us -> 11.7 us  [product(): pl.pallas_call(functools.partial(product_body, spread), in_specs=[SMEM] *...]
    unnamed x20 -> x14, local copies, waits for them, and re-layouts: 4.35 us -> 3.54 us
  transfers between devices with their start and end apart: 11 -> 11, of which waited for: 6 -> 6; matrix products, arithmetic and copies ran while one was open for 1% -> 1% of each run, Pallas kernels for 20% -> 18%
where the time goes in v3:
time: 108 us; the launch traced here: 107 us
  starting transfers between devices  53.3 us (49%)
  waiting for transfers between devices  28.4 us (26%)
  Pallas kernels  20.6 us (19%)
  local copies, waits for them, and re-layouts  4.28 us (4%)
    ppermute x6, starting transfers between devices, on_segments(): return lax.ppermute(x, SEG, pairs)  33.5 us
    ppermute x3, waiting for transfers between devices, to_layer(): lax.ppermute(x, 'rep', [(i, (i + step) % LAYERS) for i in range(LAYERS)])  20.3 us
    pallas_call x2, Pallas kernels, product(): pl.pallas_call(functools.partial(product_body, spread), in_specs=[SMEM] *...  11.7 us
    all_to_all x2, starting transfers between devices, exchange(): return lax.all_to_all(x, 'rep', 0, 0, tiled=True)  10.3 us
    ppermute x3, starting transfers between devices, to_layer(): lax.ppermute(x, 'rep', [(i, (i + step) % LAYERS) for i in range(LAYERS)])  9.57 us
    ppermute x6, waiting for transfers between devices, on_segments(): return lax.ppermute(x, SEG, pairs)  8.16 us
    unnamed x14, local copies, waits for them, and re-layouts  3.54 us
    pallas_call x1, Pallas kernels, find(): pl.pallas_call(find_body, in_specs=[SMEM] * 4, out_specs=SMEM, out_shape=...  3.27 us
  transfers between devices with their start and end apart: 11, of which 6 were waited for; matrix products, arithmetic and copies ran while one was open for 1% of the time, Pallas kernels for 18%

profile of v3, /device:TPU:35, one launch (start us, length us, event | category | flops | bytes accessed | tf_op | source)
XLA Modules:
  0.0 106.9 jit_solution(15417771745579652768)
XLA Ops:
  0.0 2.7 %collective-permute-start = (f32[2,12,128,128]{3,2,1,0:T(8,128)}, f32[2,12,128,128]{3,2,1,0:T(8,128)S(1)}, u32[]{:S(2)}, u32[]{:S(2)}) collective-permute-start(f32[2,12,128,128]{3,2,1,0:T(8,128)} %bitcast.7), channel_id=1, source_target_pairs={{0,4},{4,0},{8,12},{12,8},{16,20},{20,16},{24,28},{28,24},{32,36},... | collective-permute-start | bytes 4718600 | tf_op jit(solution)/shard_map/ppermute | solution.py:262
  2.7 0.0 copy-start.1
  2.7 1.4 %copy-done.1 = f32[2,1,12,128,128]{4,3,2,1,0:T(8,128)S(1)} copy-done((f32[2,1,12,128,128]{4,3,2,1,0:T(8,128)S(1)}, f32[2,1,12,128,128]{4,3,2,1,0:T(8,128)}, u32[]{:S(2)}) %copy-start.1) | copy-done | bytes 1572888
  4.1 1.9 %first.1 = (f32[4,2,3,128,128]{4,3,2,1,0:T(8,128)}, f32[2,12,64,128]{3,2,1,0:T(8,128)}) custom-call(f32[2,12,128,128]{3,2,1,0:T(8,128)S(1)} %bitcast.8), custom_call_target="tpu_custom_call" | custom-call | bytes 3145728 | tf_op jit(solution)/shard_map/first/pallas_call | solution.py:39
  6.0 4.0 %collective-permute-start.1 = (f32[2,12,64,128]{3,2,1,0:T(8,128)}, f32[2,12,64,128]{3,2,1,0:T(8,128)}, u32[]{:S(2)}, u32[]{:S(2)}) collective-permute-start(f32[2,12,64,128]{3,2,1,0:T(8,128)} %get-tuple-element.24.refs_0_), channel_id=1, source_target_pairs={{4,12},{8,0},{12,20},{16,8},{20,28},{24,16},{28,36},{32,24},{36,44... | collective-permute-start | bytes 2359304 | tf_op jit(solution)/shard_map/ppermute | solution.py:262
  10.0 0.0 copy-start.2
  10.0 4.7 %all-to-all-start = ((f32[4,2,3,128,128]{4,3,2,1,0:T(8,128)}), f32[4,2,3,128,128]{4,3,2,1,0:T(8,128)}, u32[]{:S(2)}, u32[]{:S(2)}) async-start(f32[4,2,3,128,128]{4,3,2,1,0:T(8,128)} %get-tuple-element.26), calls=%async_computation | async-start | bytes 3145728 | tf_op jit(solution)/shard_map/all_to_all | solution.py:274
  14.7 8.5 %collective-permute-start.2 = (f32[2,12,64,128]{3,2,1,0:T(8,128)}, f32[2,12,64,128]{3,2,1,0:T(8,128)}, u32[]{:S(2)}, u32[]{:S(2)}) collective-permute-start(f32[2,12,64,128]{3,2,1,0:T(8,128)} %get-tuple-element.24.refs_0_), channel_id=1, source_target_pairs={{0,8},{8,16},{12,4},{16,24},{20,12},{24,32},{28,20},{32,40},{36,28... | collective-permute-start | bytes 2359304 | tf_op jit(solution)/shard_map/ppermute | solution.py:262
  23.2 0.7 dynamic-slice_bitcast_fusion.near
  23.9 3.3 %find.1.where = s32[192]{0:T(256)} custom-call(s32[1]{0:T(128)} %bitcast.2.segment_ref, s32[1]{0:T(128)} %bitcast.layer_ref.layer, s32[12,40]{1,0:T(8,128)} %dynamic-slice_bitcast_fusion.near, s32[8,8]{1,0:T(8,128)} %out_cols.1), custom_call_target="tpu_custom_call" | custom-call | bytes 1048576 | tf_op jit(solution)/shard_map/find/pallas_call | solution.py:113
  27.2 3.6 %collective-permute-start.3 = (f32[2,12,64,128]{3,2,1,0:T(8,128)}, f32[2,12,64,128]{3,2,1,0:T(8,128)}, u32[]{:S(2)}, u32[]{:S(2)}) collective-permute-start(f32[2,12,64,128]{3,2,1,0:T(8,128)} %collective-permute-done.1.refs_4_), channel_id=1, source_target_pairs={{0,4},{4,0},{8,12},{12,8},{16,20},{20,16},{24,28},{28,24},{32,36},... | collective-permute-start | bytes 2359304 | tf_op jit(solution)/shard_map/ppermute | solution.py:262
  30.7 0.0 collective-permute-done.other
  30.8 0.9 later.1
  31.6 1.2 %copy-done.3 = f32[2,2,12,64,128]{4,3,2,1,0:T(8,128)} copy-done((f32[2,2,12,64,128]{4,3,2,1,0:T(8,128)}, f32[2,2,12,64,128]{4,3,2,1,0:T(8,128)S(1)}, u32[]{:S(2)}) %copy-start.3) | copy-done | bytes 1572888
  32.8 0.9 copy-done.5
  33.8 0.9 collective-permute-done.2.refs_2_
  34.7 7.7 %collective-permute-start.4 = (f32[2,2,12,64,128]{4,3,2,1,0:T(8,128)}, f32[2,2,12,64,128]{4,3,2,1,0:T(8,128)S(1)}, u32[]{:S(2)}, u32[]{:S(2)}) collective-permute-start(f32[2,2,12,64,128]{4,3,2,1,0:T(8,128)} %copy-done.3), channel_id=1, source_target_pairs={{0,8},{8,16},{12,4},{16,24},{20,12},{24,32},{28,20},{32,40},{36,28... | collective-permute-start | bytes 4718600 | tf_op jit(solution)/shard_map/ppermute | solution.py:262
  42.4 6.7 %product.1 = f32[4,2,8,64,128]{4,3,2,1,0:T(8,128)} custom-call(s32[1]{0:T(128)} %bitcast.layer_ref.layer, s32[192]{0:T(256)} %find.1.where, f32[4,2,3,128,128]{4,3,2,1,0:T(8,128)} %all-to-all-done.parts, f32[2,12,64,128]{3,2,1,0:T(8,128)} %get-tuple-element.24.refs_0_, f32[2,12,64,128]{3,2,1,0:T(8,128)} %copy-done.5, ...), custom_call_target="tpu_custom_call" | custom-call | flops 1048576 | bytes 65536 | tf_op jit(solution)/shard_map/product/pallas_call | solution.py:192
  49.1 5.6 %all-to-all-start.1 = ((f32[4,2,8,64,128]{4,3,2,1,0:T(8,128)}), f32[4,2,8,64,128]{4,3,2,1,0:T(8,128)}, u32[]{:S(2)}, u32[]{:S(2)}) async-start(f32[4,2,8,64,128]{4,3,2,1,0:T(8,128)} %product.1), calls=%async_computation.1 | async-start | bytes 4194304 | tf_op jit(solution)/shard_map/all_to_all | solution.py:274
  54.7 5.3 %collective-permute-done.4.refs_1_ = f32[2,2,12,64,128]{4,3,2,1,0:T(8,128)S(1)} collective-permute-done((f32[2,2,12,64,128]{4,3,2,1,0:T(8,128)}, f32[2,2,12,64,128]{4,3,2,1,0:T(8,128)S(1)}, u32[]{:S(2)}, u32[]{:S(2)}) %collective-permute-start.4) | collective-permute-done | bytes 1572896 | tf_op jit(solution)/shard_map/ppermute | solution.py:262
  60.0 0.1 slice_bitcast_fusion
  60.1 7.1 %collective-permute-start.5 = (f32[2,12,64,128]{3,2,1,0:T(8,128)S(1)}, f32[2,12,64,128]{3,2,1,0:T(8,128)S(1)}, u32[]{:S(2)}, u32[]{:S(2)}) collective-permute-start(f32[2,12,64,128]{3,2,1,0:T(8,128)S(1)} %slice_bitcast_fusion), channel_id=1, source_target_pairs={{0,4},{4,0},{8,12},{12,8},{16,20},{20,16},{24,28},{28,24},{32,36},... | collective-permute-start | bytes 2359304 | tf_op jit(solution)/shard_map/ppermute | solution.py:262
  67.2 1.9 %collective-permute-done.5.refs_2_ = f32[2,12,64,128]{3,2,1,0:T(8,128)S(1)} collective-permute-done((f32[2,12,64,128]{3,2,1,0:T(8,128)S(1)}, f32[2,12,64,128]{3,2,1,0:T(8,128)S(1)}, u32[]{:S(2)}, u32[]{:S(2)}) %collective-permute-start.5) | collective-permute-done | bytes 786464 | tf_op jit(solution)/shard_map/ppermute | solution.py:262
  69.1 5.0 %product_spread.1 = (f32[2,8,64,128]{3,2,1,0:T(8,128)S(1)}, f32[2,8,64,128]{3,2,1,0:T(8,128)}, f32[2,8,64,128]{3,2,1,0:T(8,128)S(1)}, f32[2,8,64,128]{3,2,1,0:T(8,128)S(1)}) custom-call(s32[1]{0:T(128)} %bitcast.layer_ref.layer, s32[192]{0:T(256)S(1)} %copy-done.6, f32[4,2,3,128,128]{4,3,2,1,0:T(8,128)} %all-to-all-done.parts, ...), custom_call_target="tpu_custom_call" | custom-call | flops 1048576 | bytes 65536 | tf_op jit(solution)/shard_map/product_spread/pallas_call | solution.py:192
  74.1 3.1 %collective-permute-start.6 = (f32[2,8,64,128]{3,2,1,0:T(8,128)}, f32[2,8,64,128]{3,2,1,0:T(8,128)S(1)}, u32[]{:S(2)}, u32[]{:S(2)}) collective-permute-start(f32[2,8,64,128]{3,2,1,0:T(8,128)} %get-tuple-element.38), channel_id=1, source_target_pairs={{0,1},{1,2},{2,3},{3,0},{4,5},{5,6},{6,7},{7,4},{8,9},{9,10},{10,1... | collective-permute-start | bytes 1572872 | tf_op jit(solution)/shard_map/ppermute | solution.py:277
  77.2 2.5 %collective-permute-start.7 = (f32[2,8,64,128]{3,2,1,0:T(8,128)S(1)}, f32[2,8,64,128]{3,2,1,0:T(8,128)S(1)}, u32[]{:S(2)}, u32[]{:S(2)}) collective-permute-start(f32[2,8,64,128]{3,2,1,0:T(8,128)S(1)} %get-tuple-element.39), channel_id=1, source_target_pairs={{0,2},{1,3},{2,0},{3,1},{4,6},{5,7},{6,4},{7,5},{8,10},{9,11},{10,... | collective-permute-start | bytes 1572872 | tf_op jit(solution)/shard_map/ppermute | solution.py:277
  79.7 4.0 %collective-permute-start.8 = (f32[2,8,64,128]{3,2,1,0:T(8,128)S(1)}, f32[2,8,64,128]{3,2,1,0:T(8,128)S(1)}, u32[]{:S(2)}, u32[]{:S(2)}) collective-permute-start(f32[2,8,64,128]{3,2,1,0:T(8,128)S(1)} %get-tuple-element.40), channel_id=1, source_target_pairs={{0,3},{1,0},{2,1},{3,2},{4,7},{5,4},{6,5},{7,6},{8,11},{9,8},{10,9... | collective-permute-start | bytes 1572872 | tf_op jit(solution)/shard_map/ppermute | solution.py:277
  83.7 1.7 %add_first.1.half0 = f32[2,8,64,128]{3,2,1,0:T(8,128)S(1)} custom-call(f32[4,2,8,64,128]{4,3,2,1,0:T(8,128)} %all-to-all-done.1.shares), custom_call_target="tpu_custom_call" | custom-call | bytes 3145728 | tf_op jit(solution)/shard_map/add_first/pallas_call | solution.py:218
  85.4 3.9 %collective-permute-done.6.share1 = f32[2,8,64,128]{3,2,1,0:T(8,128)S(1)} collective-permute-done((f32[2,8,64,128]{3,2,1,0:T(8,128)}, f32[2,8,64,128]{3,2,1,0:T(8,128)S(1)}, u32[]{:S(2)}, u32[]{:S(2)}) %collective-permute-start.6) | collective-permute-done | bytes 524320 | tf_op jit(solution)/shard_map/ppermute | solution.py:277
  89.3 4.1 %collective-permute-done.7.share2 = f32[2,8,64,128]{3,2,1,0:T(8,128)S(1)} collective-permute-done((f32[2,8,64,128]{3,2,1,0:T(8,128)S(1)}, f32[2,8,64,128]{3,2,1,0:T(8,128)S(1)}, u32[]{:S(2)}, u32[]{:S(2)}) %collective-permute-start.7) | collective-permute-done | bytes 524320 | tf_op jit(solution)/shard_map/ppermute | solution.py:277
  93.4 12.2 %collective-permute-done.8.share3 = f32[2,8,64,128]{3,2,1,0:T(8,128)S(1)} collective-permute-done((f32[2,8,64,128]{3,2,1,0:T(8,128)S(1)}, f32[2,8,64,128]{3,2,1,0:T(8,128)S(1)}, u32[]{:S(2)}, u32[]{:S(2)}) %collective-permute-start.8) | collective-permute-done | bytes 524320 | tf_op jit(solution)/shard_map/ppermute | solution.py:277
  105.7 1.2 %add_last.1 = f32[2,8,128,128]{3,2,1,0:T(8,128)} custom-call(f32[2,8,64,128]{3,2,1,0:T(8,128)S(1)} %add_first.1.half0, f32[2,8,64,128]{3,2,1,0:T(8,128)S(1)} %get-tuple-element.37.share0, f32[2,8,64,128]{3,2,1,0:T(8,128)S(1)} %collective-permute-done.6.share1, f32[2,8,64,128]{3,2,1,0:T(8,128)S(1)} %collective-permute-done.7.share2, ...), custom_call_target="tpu_custom_call" | custom-call | bytes 4194304 | tf_op jit(solution)/shard_map/add_last/pallas_call | solution.py:238
  (13 shorter events, 0.0 us)
Async XLA Ops:
  0.0 23.2 %copy-start = (s32[1024,12]{0,1:T(8,128)S(1)}, s32[1024,12]{0,1:T(8,128)}, u32[]{:S(2)}) copy-start(s32[1024,12]{0,1:T(8,128)} %param.4) | copy-start | bytes 147460
  0.0 30.7 %collective-permute-start = (f32[2,12,128,128]{3,2,1,0:T(8,128)}, f32[2,12,128,128]{3,2,1,0:T(8,128)S(1)}, u32[]{:S(2)}, u32[]{:S(2)}) collective-permute-start(f32[2,12,128,128]{3,2,1,0:T(8,128)} %bitcast.7), channel_id=1, source_target_pairs={{0,4},{4,0},{8,12},{12,8},{16,20},{20,16},{24,28},{28,24},{32,36},... | collective-permute-start | bytes 4718600 | tf_op jit(solution)/shard_map/ppermute | solution.py:262
  2.7 1.4 %copy-start.1 = (f32[2,1,12,128,128]{4,3,2,1,0:T(8,128)S(1)}, f32[2,1,12,128,128]{4,3,2,1,0:T(8,128)}, u32[]{:S(2)}) copy-start(f32[2,1,12,128,128]{4,3,2,1,0:T(8,128)} %param.3) | copy-start | bytes 4718596
  6.0 21.2 %collective-permute-start.1 = (f32[2,12,64,128]{3,2,1,0:T(8,128)}, f32[2,12,64,128]{3,2,1,0:T(8,128)}, u32[]{:S(2)}, u32[]{:S(2)}) collective-permute-start(f32[2,12,64,128]{3,2,1,0:T(8,128)} %get-tuple-element.24.refs_0_), channel_id=1, source_target_pairs={{4,12},{8,0},{12,20},{16,8},{20,28},{24,16},{28,36},{32,24},{36,44... | collective-permute-start | bytes 2359304 | tf_op jit(solution)/shard_map/ppermute | solution.py:262
  10.0 20.8 %copy-start.2 = (f32[2,1,12,128,128]{4,3,2,1,0:T(8,128)S(1)}, f32[2,1,12,128,128]{4,3,2,1,0:T(8,128)}, u32[]{:S(2)}) copy-start(f32[2,1,12,128,128]{4,3,2,1,0:T(8,128)} %param.3) | copy-start | bytes 4718596
  10.0 24.7 %all-to-all-start = ((f32[4,2,3,128,128]{4,3,2,1,0:T(8,128)}), f32[4,2,3,128,128]{4,3,2,1,0:T(8,128)}, u32[]{:S(2)}, u32[]{:S(2)}) async-start(f32[4,2,3,128,128]{4,3,2,1,0:T(8,128)} %get-tuple-element.26), calls=%async_computation | async-start | bytes 3145728 | tf_op jit(solution)/shard_map/all_to_all | solution.py:274
  14.7 20.0 %collective-permute-start.2 = (f32[2,12,64,128]{3,2,1,0:T(8,128)}, f32[2,12,64,128]{3,2,1,0:T(8,128)}, u32[]{:S(2)}, u32[]{:S(2)}) collective-permute-start(f32[2,12,64,128]{3,2,1,0:T(8,128)} %get-tuple-element.24.refs_0_), channel_id=1, source_target_pairs={{0,8},{8,16},{12,4},{16,24},{20,12},{24,32},{28,20},{32,40},{36,28... | collective-permute-start | bytes 2359304 | tf_op jit(solution)/shard_map/ppermute | solution.py:262
  27.2 7.5 %collective-permute-start.3 = (f32[2,12,64,128]{3,2,1,0:T(8,128)}, f32[2,12,64,128]{3,2,1,0:T(8,128)}, u32[]{:S(2)}, u32[]{:S(2)}) collective-permute-start(f32[2,12,64,128]{3,2,1,0:T(8,128)} %collective-permute-done.1.refs_4_), channel_id=1, source_target_pairs={{0,4},{4,0},{8,12},{12,8},{16,20},{20,16},{24,28},{28,24},{32,36},... | collective-permute-start | bytes 2359304 | tf_op jit(solution)/shard_map/ppermute | solution.py:262
  31.6 1.2 %copy-start.3 = (f32[2,2,12,64,128]{4,3,2,1,0:T(8,128)}, f32[2,2,12,64,128]{4,3,2,1,0:T(8,128)S(1)}, u32[]{:S(2)}) copy-start(f32[2,2,12,64,128]{4,3,2,1,0:T(8,128)S(1)} %get-tuple-element.34.refs_0_) | copy-start | bytes 4718596
  32.8 0.9 copy-start.5
  34.7 25.4 %collective-permute-start.4 = (f32[2,2,12,64,128]{4,3,2,1,0:T(8,128)}, f32[2,2,12,64,128]{4,3,2,1,0:T(8,128)S(1)}, u32[]{:S(2)}, u32[]{:S(2)}) collective-permute-start(f32[2,2,12,64,128]{4,3,2,1,0:T(8,128)} %copy-done.3), channel_id=1, source_target_pairs={{0,8},{8,16},{12,4},{16,24},{20,12},{24,32},{28,20},{32,40},{36,28... | collective-permute-start | bytes 4718600 | tf_op jit(solution)/shard_map/ppermute | solution.py:262
  49.1 20.0 %copy-start.6 = (s32[192]{0:T(256)S(1)}, s32[192]{0:T(256)}, u32[]{:S(2)}) copy-start(s32[192]{0:T(256)} %find.1.where) | copy-start | bytes 2308
  49.1 34.6 %all-to-all-start.1 = ((f32[4,2,8,64,128]{4,3,2,1,0:T(8,128)}), f32[4,2,8,64,128]{4,3,2,1,0:T(8,128)}, u32[]{:S(2)}, u32[]{:S(2)}) async-start(f32[4,2,8,64,128]{4,3,2,1,0:T(8,128)} %product.1), calls=%async_computation.1 | async-start | bytes 4194304 | tf_op jit(solution)/shard_map/all_to_all | solution.py:274
  54.7 14.4 %copy-start.4 = (f32[2,2,12,64,128]{4,3,2,1,0:T(8,128)S(1)}, f32[2,2,12,64,128]{4,3,2,1,0:T(8,128)}, u32[]{:S(2)}) copy-start(f32[2,2,12,64,128]{4,3,2,1,0:T(8,128)} %copy-done.3) | copy-start | bytes 4718596
  60.1 9.0 %collective-permute-start.5 = (f32[2,12,64,128]{3,2,1,0:T(8,128)S(1)}, f32[2,12,64,128]{3,2,1,0:T(8,128)S(1)}, u32[]{:S(2)}, u32[]{:S(2)}) collective-permute-start(f32[2,12,64,128]{3,2,1,0:T(8,128)S(1)} %slice_bitcast_fusion), channel_id=1, source_target_pairs={{0,4},{4,0},{8,12},{12,8},{16,20},{20,16},{24,28},{28,24},{32,36},... | collective-permute-start | bytes 2359304 | tf_op jit(solution)/shard_map/ppermute | solution.py:262
  74.1 15.2 %collective-permute-start.6 = (f32[2,8,64,128]{3,2,1,0:T(8,128)}, f32[2,8,64,128]{3,2,1,0:T(8,128)S(1)}, u32[]{:S(2)}, u32[]{:S(2)}) collective-permute-start(f32[2,8,64,128]{3,2,1,0:T(8,128)} %get-tuple-element.38), channel_id=1, source_target_pairs={{0,1},{1,2},{2,3},{3,0},{4,5},{5,6},{6,7},{7,4},{8,9},{9,10},{10,1... | collective-permute-start | bytes 1572872 | tf_op jit(solution)/shard_map/ppermute | solution.py:277
  77.2 16.2 %collective-permute-start.7 = (f32[2,8,64,128]{3,2,1,0:T(8,128)S(1)}, f32[2,8,64,128]{3,2,1,0:T(8,128)S(1)}, u32[]{:S(2)}, u32[]{:S(2)}) collective-permute-start(f32[2,8,64,128]{3,2,1,0:T(8,128)S(1)} %get-tuple-element.39), channel_id=1, source_target_pairs={{0,2},{1,3},{2,0},{3,1},{4,6},{5,7},{6,4},{7,5},{8,10},{9,11},{10,... | collective-permute-start | bytes 1572872 | tf_op jit(solution)/shard_map/ppermute | solution.py:277
  79.7 25.9 %collective-permute-start.8 = (f32[2,8,64,128]{3,2,1,0:T(8,128)S(1)}, f32[2,8,64,128]{3,2,1,0:T(8,128)S(1)}, u32[]{:S(2)}, u32[]{:S(2)}) collective-permute-start(f32[2,8,64,128]{3,2,1,0:T(8,128)S(1)} %get-tuple-element.40), channel_id=1, source_target_pairs={{0,3},{1,0},{2,1},{3,2},{4,7},{5,4},{6,5},{7,6},{8,11},{9,8},{10,9... | collective-permute-start | bytes 1572872 | tf_op jit(solution)/shard_map/ppermute | solution.py:277

commit v4 on v3

--- a/solution.py
+++ b/solution.py
@@ -298,7 +298,7 @@
     received1 = [kept1] + [None] * 3
     for step in (2, 1, 3):
         received1[step] = to_layer(shares1[step], step)
-    return add_last(add_first(received0), received1)
+    return add_last(add_first(received0), [received1[step] for step in (0, 2, 1, 3)])
 
 
 def solution(mesh):

time: 108 us -> 105 us (0.972)
  waiting for transfers between devices: 28.4 us -> 26.1 us
    ppermute x3, waiting for transfers between devices: 20.3 us -> 18 us  [to_layer(): lax.ppermute(x, 'rep', [(i, (i + step) % LAYERS) for i in range(LAYERS)])]
  transfers between devices with their start and end apart: 11 -> 11, of which waited for: 6 -> 6; matrix products, arithmetic and copies ran while one was open for 1% -> 1% of each run, Pallas kernels for 18% -> 19%
where the time goes in v4:
time: 105 us; the launch traced here: 104 us
  starting transfers between devices  52.7 us (50%)
  waiting for transfers between devices  26.1 us (25%)
  Pallas kernels  20.6 us (20%)
  local copies, waits for them, and re-layouts  4.28 us (4%)
    ppermute x6, starting transfers between devices, on_segments(): return lax.ppermute(x, SEG, pairs)  33.5 us
    ppermute x3, waiting for transfers between devices, to_layer(): lax.ppermute(x, 'rep', [(i, (i + step) % LAYERS) for i in range(LAYERS)])  18 us
    pallas_call x2, Pallas kernels, product(): pl.pallas_call(functools.partial(product_body, spread), in_specs=[SMEM] *...  11.7 us
    all_to_all x2, starting transfers between devices, exchange(): return lax.all_to_all(x, 'rep', 0, 0, tiled=True)  10.3 us
    ppermute x3, starting transfers between devices, to_layer(): lax.ppermute(x, 'rep', [(i, (i + step) % LAYERS) for i in range(LAYERS)])  8.99 us
    ppermute x6, waiting for transfers between devices, on_segments(): return lax.ppermute(x, SEG, pairs)  8.16 us
    unnamed x14, local copies, waits for them, and re-layouts  3.54 us
    pallas_call x1, Pallas kernels, find(): pl.pallas_call(find_body, in_specs=[SMEM] * 4, out_specs=SMEM, out_shape=...  3.27 us
  transfers between devices with their start and end apart: 11, of which 6 were waited for; matrix products, arithmetic and copies ran while one was open for 1% of the time, Pallas kernels for 19%

profile of v4, /device:TPU:35, one launch (start us, length us, event | category | flops | bytes accessed | tf_op | source)
XLA Modules:
  0.0 104.0 jit_solution(4258621148344493058)
XLA Ops:
  0.0 2.7 %collective-permute-start = (f32[2,12,128,128]{3,2,1,0:T(8,128)}, f32[2,12,128,128]{3,2,1,0:T(8,128)S(1)}, u32[]{:S(2)}, u32[]{:S(2)}) collective-permute-start(f32[2,12,128,128]{3,2,1,0:T(8,128)} %bitcast.7), channel_id=1, source_target_pairs={{0,4},{4,0},{8,12},{12,8},{16,20},{20,16},{24,28},{28,24},{32,36},... | collective-permute-start | bytes 4718600 | tf_op jit(solution)/shard_map/ppermute | solution.py:262
  2.7 0.0 copy-start.1
  2.7 1.4 %copy-done.1 = f32[2,1,12,128,128]{4,3,2,1,0:T(8,128)S(1)} copy-done((f32[2,1,12,128,128]{4,3,2,1,0:T(8,128)S(1)}, f32[2,1,12,128,128]{4,3,2,1,0:T(8,128)}, u32[]{:S(2)}) %copy-start.1) | copy-done | bytes 1572888
  4.1 1.9 %first.1 = (f32[4,2,3,128,128]{4,3,2,1,0:T(8,128)}, f32[2,12,64,128]{3,2,1,0:T(8,128)}) custom-call(f32[2,12,128,128]{3,2,1,0:T(8,128)S(1)} %bitcast.8), custom_call_target="tpu_custom_call" | custom-call | bytes 3145728 | tf_op jit(solution)/shard_map/first/pallas_call | solution.py:39
  6.0 4.0 %collective-permute-start.1 = (f32[2,12,64,128]{3,2,1,0:T(8,128)}, f32[2,12,64,128]{3,2,1,0:T(8,128)}, u32[]{:S(2)}, u32[]{:S(2)}) collective-permute-start(f32[2,12,64,128]{3,2,1,0:T(8,128)} %get-tuple-element.24.refs_0_), channel_id=1, source_target_pairs={{4,12},{8,0},{12,20},{16,8},{20,28},{24,16},{28,36},{32,24},{36,44... | collective-permute-start | bytes 2359304 | tf_op jit(solution)/shard_map/ppermute | solution.py:262
  10.0 0.0 copy-start.2
  10.0 4.7 %all-to-all-start = ((f32[4,2,3,128,128]{4,3,2,1,0:T(8,128)}), f32[4,2,3,128,128]{4,3,2,1,0:T(8,128)}, u32[]{:S(2)}, u32[]{:S(2)}) async-start(f32[4,2,3,128,128]{4,3,2,1,0:T(8,128)} %get-tuple-element.26), calls=%async_computation | async-start | bytes 3145728 | tf_op jit(solution)/shard_map/all_to_all | solution.py:274
  14.7 8.5 %collective-permute-start.2 = (f32[2,12,64,128]{3,2,1,0:T(8,128)}, f32[2,12,64,128]{3,2,1,0:T(8,128)}, u32[]{:S(2)}, u32[]{:S(2)}) collective-permute-start(f32[2,12,64,128]{3,2,1,0:T(8,128)} %get-tuple-element.24.refs_0_), channel_id=1, source_target_pairs={{0,8},{8,16},{12,4},{16,24},{20,12},{24,32},{28,20},{32,40},{36,28... | collective-permute-start | bytes 2359304 | tf_op jit(solution)/shard_map/ppermute | solution.py:262
  23.2 0.7 dynamic-slice_bitcast_fusion.near
  23.9 3.3 %find.1.where = s32[192]{0:T(256)} custom-call(s32[1]{0:T(128)} %bitcast.2.segment_ref, s32[1]{0:T(128)} %bitcast.layer_ref.layer, s32[12,40]{1,0:T(8,128)} %dynamic-slice_bitcast_fusion.near, s32[8,8]{1,0:T(8,128)} %out_cols.1), custom_call_target="tpu_custom_call" | custom-call | bytes 1048576 | tf_op jit(solution)/shard_map/find/pallas_call | solution.py:113
  27.2 0.0 collective-permute-done.1.refs_4_
  27.2 3.6 %collective-permute-start.3 = (f32[2,12,64,128]{3,2,1,0:T(8,128)}, f32[2,12,64,128]{3,2,1,0:T(8,128)}, u32[]{:S(2)}, u32[]{:S(2)}) collective-permute-start(f32[2,12,64,128]{3,2,1,0:T(8,128)} %collective-permute-done.1.refs_4_), channel_id=1, source_target_pairs={{0,4},{4,0},{8,12},{12,8},{16,20},{20,16},{24,28},{28,24},{32,36},... | collective-permute-start | bytes 2359304 | tf_op jit(solution)/shard_map/ppermute | solution.py:262
  30.8 0.9 later.1
  31.6 1.2 %copy-done.3 = f32[2,2,12,64,128]{4,3,2,1,0:T(8,128)} copy-done((f32[2,2,12,64,128]{4,3,2,1,0:T(8,128)}, f32[2,2,12,64,128]{4,3,2,1,0:T(8,128)S(1)}, u32[]{:S(2)}) %copy-start.3) | copy-done | bytes 1572888
  32.8 0.9 copy-done.5
  33.8 0.9 collective-permute-done.2.refs_2_
  34.7 7.7 %collective-permute-start.4 = (f32[2,2,12,64,128]{4,3,2,1,0:T(8,128)}, f32[2,2,12,64,128]{4,3,2,1,0:T(8,128)S(1)}, u32[]{:S(2)}, u32[]{:S(2)}) collective-permute-start(f32[2,2,12,64,128]{4,3,2,1,0:T(8,128)} %copy-done.3), channel_id=1, source_target_pairs={{0,8},{8,16},{12,4},{16,24},{20,12},{24,32},{28,20},{32,40},{36,28... | collective-permute-start | bytes 4718600 | tf_op jit(solution)/shard_map/ppermute | solution.py:262
  42.4 6.7 %product.1 = f32[4,2,8,64,128]{4,3,2,1,0:T(8,128)} custom-call(s32[1]{0:T(128)} %bitcast.layer_ref.layer, s32[192]{0:T(256)} %find.1.where, f32[4,2,3,128,128]{4,3,2,1,0:T(8,128)} %all-to-all-done.parts, f32[2,12,64,128]{3,2,1,0:T(8,128)} %get-tuple-element.24.refs_0_, f32[2,12,64,128]{3,2,1,0:T(8,128)} %copy-done.5, ...), custom_call_target="tpu_custom_call" | custom-call | flops 1048576 | bytes 65536 | tf_op jit(solution)/shard_map/product/pallas_call | solution.py:192
  49.1 5.6 %all-to-all-start.1 = ((f32[4,2,8,64,128]{4,3,2,1,0:T(8,128)}), f32[4,2,8,64,128]{4,3,2,1,0:T(8,128)}, u32[]{:S(2)}, u32[]{:S(2)}) async-start(f32[4,2,8,64,128]{4,3,2,1,0:T(8,128)} %product.1), calls=%async_computation.1 | async-start | bytes 4194304 | tf_op jit(solution)/shard_map/all_to_all | solution.py:274
  54.7 5.3 %collective-permute-done.4.refs_1_ = f32[2,2,12,64,128]{4,3,2,1,0:T(8,128)S(1)} collective-permute-done((f32[2,2,12,64,128]{4,3,2,1,0:T(8,128)}, f32[2,2,12,64,128]{4,3,2,1,0:T(8,128)S(1)}, u32[]{:S(2)}, u32[]{:S(2)}) %collective-permute-start.4) | collective-permute-done | bytes 1572896 | tf_op jit(solution)/shard_map/ppermute | solution.py:262
  60.0 0.1 slice_bitcast_fusion
  60.1 7.1 %collective-permute-start.5 = (f32[2,12,64,128]{3,2,1,0:T(8,128)S(1)}, f32[2,12,64,128]{3,2,1,0:T(8,128)S(1)}, u32[]{:S(2)}, u32[]{:S(2)}) collective-permute-start(f32[2,12,64,128]{3,2,1,0:T(8,128)S(1)} %slice_bitcast_fusion), channel_id=1, source_target_pairs={{0,4},{4,0},{8,12},{12,8},{16,20},{20,16},{24,28},{28,24},{32,36},... | collective-permute-start | bytes 2359304 | tf_op jit(solution)/shard_map/ppermute | solution.py:262
  67.2 1.9 %collective-permute-done.5.refs_2_ = f32[2,12,64,128]{3,2,1,0:T(8,128)S(1)} collective-permute-done((f32[2,12,64,128]{3,2,1,0:T(8,128)S(1)}, f32[2,12,64,128]{3,2,1,0:T(8,128)S(1)}, u32[]{:S(2)}, u32[]{:S(2)}) %collective-permute-start.5) | collective-permute-done | bytes 786464 | tf_op jit(solution)/shard_map/ppermute | solution.py:262
  69.1 5.0 %product_spread.1 = (f32[2,8,64,128]{3,2,1,0:T(8,128)S(1)}, f32[2,8,64,128]{3,2,1,0:T(8,128)S(1)}, f32[2,8,64,128]{3,2,1,0:T(8,128)}, f32[2,8,64,128]{3,2,1,0:T(8,128)S(1)}) custom-call(s32[1]{0:T(128)} %bitcast.layer_ref.layer, s32[192]{0:T(256)S(1)} %copy-done.6, f32[4,2,3,128,128]{4,3,2,1,0:T(8,128)} %all-to-all-done.parts, ...), custom_call_target="tpu_custom_call" | custom-call | flops 1048576 | bytes 65536 | tf_op jit(solution)/shard_map/product_spread/pallas_call | solution.py:192
  74.1 3.7 %collective-permute-start.6 = (f32[2,8,64,128]{3,2,1,0:T(8,128)}, f32[2,8,64,128]{3,2,1,0:T(8,128)S(1)}, u32[]{:S(2)}, u32[]{:S(2)}) collective-permute-start(f32[2,8,64,128]{3,2,1,0:T(8,128)} %get-tuple-element.38), channel_id=1, source_target_pairs={{0,2},{1,3},{2,0},{3,1},{4,6},{5,7},{6,4},{7,5},{8,10},{9,11},{10,... | collective-permute-start | bytes 1572872 | tf_op jit(solution)/shard_map/ppermute | solution.py:277
  77.8 1.9 %collective-permute-start.7 = (f32[2,8,64,128]{3,2,1,0:T(8,128)S(1)}, f32[2,8,64,128]{3,2,1,0:T(8,128)S(1)}, u32[]{:S(2)}, u32[]{:S(2)}) collective-permute-start(f32[2,8,64,128]{3,2,1,0:T(8,128)S(1)} %get-tuple-element.39), channel_id=1, source_target_pairs={{0,1},{1,2},{2,3},{3,0},{4,5},{5,6},{6,7},{7,4},{8,9},{9,10},{10,1... | collective-permute-start | bytes 1572872 | tf_op jit(solution)/shard_map/ppermute | solution.py:277
  79.7 3.4 %collective-permute-start.8 = (f32[2,8,64,128]{3,2,1,0:T(8,128)S(1)}, f32[2,8,64,128]{3,2,1,0:T(8,128)S(1)}, u32[]{:S(2)}, u32[]{:S(2)}) collective-permute-start(f32[2,8,64,128]{3,2,1,0:T(8,128)S(1)} %get-tuple-element.40), channel_id=1, source_target_pairs={{0,3},{1,0},{2,1},{3,2},{4,7},{5,4},{6,5},{7,6},{8,11},{9,8},{10,9... | collective-permute-start | bytes 1572872 | tf_op jit(solution)/shard_map/ppermute | solution.py:277
  83.1 1.7 %add_first.1.half0 = f32[2,8,64,128]{3,2,1,0:T(8,128)S(1)} custom-call(f32[4,2,8,64,128]{4,3,2,1,0:T(8,128)} %all-to-all-done.1.shares), custom_call_target="tpu_custom_call" | custom-call | bytes 3145728 | tf_op jit(solution)/shard_map/add_first/pallas_call | solution.py:218
  84.8 6.1 %collective-permute-done.6.share1 = f32[2,8,64,128]{3,2,1,0:T(8,128)S(1)} collective-permute-done((f32[2,8,64,128]{3,2,1,0:T(8,128)}, f32[2,8,64,128]{3,2,1,0:T(8,128)S(1)}, u32[]{:S(2)}, u32[]{:S(2)}) %collective-permute-start.6) | collective-permute-done | bytes 524320 | tf_op jit(solution)/shard_map/ppermute | solution.py:277
  90.9 11.2 %collective-permute-done.7.share2 = f32[2,8,64,128]{3,2,1,0:T(8,128)S(1)} collective-permute-done((f32[2,8,64,128]{3,2,1,0:T(8,128)S(1)}, f32[2,8,64,128]{3,2,1,0:T(8,128)S(1)}, u32[]{:S(2)}, u32[]{:S(2)}) %collective-permute-start.7) | collective-permute-done | bytes 524320 | tf_op jit(solution)/shard_map/ppermute | solution.py:277
  102.1 0.7 collective-permute-done.8.share3
  102.8 1.2 %add_last.1 = f32[2,8,128,128]{3,2,1,0:T(8,128)} custom-call(f32[2,8,64,128]{3,2,1,0:T(8,128)S(1)} %add_first.1.half0, f32[2,8,64,128]{3,2,1,0:T(8,128)S(1)} %get-tuple-element.37.share0, f32[2,8,64,128]{3,2,1,0:T(8,128)S(1)} %collective-permute-done.6.share1, f32[2,8,64,128]{3,2,1,0:T(8,128)S(1)} %collective-permute-done.7.share2, ...), custom_call_target="tpu_custom_call" | custom-call | bytes 4194304 | tf_op jit(solution)/shard_map/add_last/pallas_call | solution.py:238
  (13 shorter events, 0.0 us)
Async XLA Ops:
  0.0 23.2 %copy-start = (s32[1024,12]{0,1:T(8,128)S(1)}, s32[1024,12]{0,1:T(8,128)}, u32[]{:S(2)}) copy-start(s32[1024,12]{0,1:T(8,128)} %param.4) | copy-start | bytes 147460
  0.0 30.7 %collective-permute-start = (f32[2,12,128,128]{3,2,1,0:T(8,128)}, f32[2,12,128,128]{3,2,1,0:T(8,128)S(1)}, u32[]{:S(2)}, u32[]{:S(2)}) collective-permute-start(f32[2,12,128,128]{3,2,1,0:T(8,128)} %bitcast.7), channel_id=1, source_target_pairs={{0,4},{4,0},{8,12},{12,8},{16,20},{20,16},{24,28},{28,24},{32,36},... | collective-permute-start | bytes 4718600 | tf_op jit(solution)/shard_map/ppermute | solution.py:262
  2.7 1.4 %copy-start.1 = (f32[2,1,12,128,128]{4,3,2,1,0:T(8,128)S(1)}, f32[2,1,12,128,128]{4,3,2,1,0:T(8,128)}, u32[]{:S(2)}) copy-start(f32[2,1,12,128,128]{4,3,2,1,0:T(8,128)} %param.3) | copy-start | bytes 4718596
  6.0 21.2 %collective-permute-start.1 = (f32[2,12,64,128]{3,2,1,0:T(8,128)}, f32[2,12,64,128]{3,2,1,0:T(8,128)}, u32[]{:S(2)}, u32[]{:S(2)}) collective-permute-start(f32[2,12,64,128]{3,2,1,0:T(8,128)} %get-tuple-element.24.refs_0_), channel_id=1, source_target_pairs={{4,12},{8,0},{12,20},{16,8},{20,28},{24,16},{28,36},{32,24},{36,44... | collective-permute-start | bytes 2359304 | tf_op jit(solution)/shard_map/ppermute | solution.py:262
  10.0 20.8 %copy-start.2 = (f32[2,1,12,128,128]{4,3,2,1,0:T(8,128)S(1)}, f32[2,1,12,128,128]{4,3,2,1,0:T(8,128)}, u32[]{:S(2)}) copy-start(f32[2,1,12,128,128]{4,3,2,1,0:T(8,128)} %param.3) | copy-start | bytes 4718596
  10.0 24.7 %all-to-all-start = ((f32[4,2,3,128,128]{4,3,2,1,0:T(8,128)}), f32[4,2,3,128,128]{4,3,2,1,0:T(8,128)}, u32[]{:S(2)}, u32[]{:S(2)}) async-start(f32[4,2,3,128,128]{4,3,2,1,0:T(8,128)} %get-tuple-element.26), calls=%async_computation | async-start | bytes 3145728 | tf_op jit(solution)/shard_map/all_to_all | solution.py:274
  14.7 20.0 %collective-permute-start.2 = (f32[2,12,64,128]{3,2,1,0:T(8,128)}, f32[2,12,64,128]{3,2,1,0:T(8,128)}, u32[]{:S(2)}, u32[]{:S(2)}) collective-permute-start(f32[2,12,64,128]{3,2,1,0:T(8,128)} %get-tuple-element.24.refs_0_), channel_id=1, source_target_pairs={{0,8},{8,16},{12,4},{16,24},{20,12},{24,32},{28,20},{32,40},{36,28... | collective-permute-start | bytes 2359304 | tf_op jit(solution)/shard_map/ppermute | solution.py:262
  27.2 7.5 %collective-permute-start.3 = (f32[2,12,64,128]{3,2,1,0:T(8,128)}, f32[2,12,64,128]{3,2,1,0:T(8,128)}, u32[]{:S(2)}, u32[]{:S(2)}) collective-permute-start(f32[2,12,64,128]{3,2,1,0:T(8,128)} %collective-permute-done.1.refs_4_), channel_id=1, source_target_pairs={{0,4},{4,0},{8,12},{12,8},{16,20},{20,16},{24,28},{28,24},{32,36},... | collective-permute-start | bytes 2359304 | tf_op jit(solution)/shard_map/ppermute | solution.py:262
  31.6 1.2 %copy-start.3 = (f32[2,2,12,64,128]{4,3,2,1,0:T(8,128)}, f32[2,2,12,64,128]{4,3,2,1,0:T(8,128)S(1)}, u32[]{:S(2)}) copy-start(f32[2,2,12,64,128]{4,3,2,1,0:T(8,128)S(1)} %get-tuple-element.34.refs_0_) | copy-start | bytes 4718596
  32.8 0.9 copy-start.5
  34.7 25.4 %collective-permute-start.4 = (f32[2,2,12,64,128]{4,3,2,1,0:T(8,128)}, f32[2,2,12,64,128]{4,3,2,1,0:T(8,128)S(1)}, u32[]{:S(2)}, u32[]{:S(2)}) collective-permute-start(f32[2,2,12,64,128]{4,3,2,1,0:T(8,128)} %copy-done.3), channel_id=1, source_target_pairs={{0,8},{8,16},{12,4},{16,24},{20,12},{24,32},{28,20},{32,40},{36,28... | collective-permute-start | bytes 4718600 | tf_op jit(solution)/shard_map/ppermute | solution.py:262
  49.1 20.0 %copy-start.6 = (s32[192]{0:T(256)S(1)}, s32[192]{0:T(256)}, u32[]{:S(2)}) copy-start(s32[192]{0:T(256)} %find.1.where) | copy-start | bytes 2308
  49.1 34.0 %all-to-all-start.1 = ((f32[4,2,8,64,128]{4,3,2,1,0:T(8,128)}), f32[4,2,8,64,128]{4,3,2,1,0:T(8,128)}, u32[]{:S(2)}, u32[]{:S(2)}) async-start(f32[4,2,8,64,128]{4,3,2,1,0:T(8,128)} %product.1), calls=%async_computation.1 | async-start | bytes 4194304 | tf_op jit(solution)/shard_map/all_to_all | solution.py:274
  54.7 14.4 %copy-start.4 = (f32[2,2,12,64,128]{4,3,2,1,0:T(8,128)S(1)}, f32[2,2,12,64,128]{4,3,2,1,0:T(8,128)}, u32[]{:S(2)}) copy-start(f32[2,2,12,64,128]{4,3,2,1,0:T(8,128)} %copy-done.3) | copy-start | bytes 4718596
  60.1 9.0 %collective-permute-start.5 = (f32[2,12,64,128]{3,2,1,0:T(8,128)S(1)}, f32[2,12,64,128]{3,2,1,0:T(8,128)S(1)}, u32[]{:S(2)}, u32[]{:S(2)}) collective-permute-start(f32[2,12,64,128]{3,2,1,0:T(8,128)S(1)} %slice_bitcast_fusion), channel_id=1, source_target_pairs={{0,4},{4,0},{8,12},{12,8},{16,20},{20,16},{24,28},{28,24},{32,36},... | collective-permute-start | bytes 2359304 | tf_op jit(solution)/shard_map/ppermute | solution.py:262
  74.1 16.8 %collective-permute-start.6 = (f32[2,8,64,128]{3,2,1,0:T(8,128)}, f32[2,8,64,128]{3,2,1,0:T(8,128)S(1)}, u32[]{:S(2)}, u32[]{:S(2)}) collective-permute-start(f32[2,8,64,128]{3,2,1,0:T(8,128)} %get-tuple-element.38), channel_id=1, source_target_pairs={{0,2},{1,3},{2,0},{3,1},{4,6},{5,7},{6,4},{7,5},{8,10},{9,11},{10,... | collective-permute-start | bytes 1572872 | tf_op jit(solution)/shard_map/ppermute | solution.py:277
  77.8 24.3 %collective-permute-start.7 = (f32[2,8,64,128]{3,2,1,0:T(8,128)S(1)}, f32[2,8,64,128]{3,2,1,0:T(8,128)S(1)}, u32[]{:S(2)}, u32[]{:S(2)}) collective-permute-start(f32[2,8,64,128]{3,2,1,0:T(8,128)S(1)} %get-tuple-element.39), channel_id=1, source_target_pairs={{0,1},{1,2},{2,3},{3,0},{4,5},{5,6},{6,7},{7,4},{8,9},{9,10},{10,1... | collective-permute-start | bytes 1572872 | tf_op jit(solution)/shard_map/ppermute | solution.py:277
  79.7 23.0 %collective-permute-start.8 = (f32[2,8,64,128]{3,2,1,0:T(8,128)S(1)}, f32[2,8,64,128]{3,2,1,0:T(8,128)S(1)}, u32[]{:S(2)}, u32[]{:S(2)}) collective-permute-start(f32[2,8,64,128]{3,2,1,0:T(8,128)S(1)} %get-tuple-element.40), channel_id=1, source_target_pairs={{0,3},{1,0},{2,1},{3,2},{4,7},{5,4},{6,5},{7,6},{8,11},{9,8},{10,9... | collective-permute-start | bytes 1572872 | tf_op jit(solution)/shard_map/ppermute | solution.py:277
